TPU v7x, 128 devices: a whole 4x4x4 slice. The times are simulated.
128 devices in a mesh: group: 16 (over y, z), fold: 8 (over x, core).
Axes of the slice: x: 4, y: 4, z: 4, core: 2. Of those that a mesh axis runs over, the one named last changes fastest.
Arguments:
- right_side: float32 [16, 262144], P(None, ('group', 'fold')), may hold values from -6 to 6
- initial: float32 [16, 262144], P(None, ('group', 'fold')), may hold values from -6 to 6
- counts: int32 [16, 8], P('group'), may hold values from 1 to 2048, 8192 in all within a row
- columns: int32 [1024, 5], P('group'), may hold values from 0 to 69, as said below
- blocks: float32 [1024, 5, 128, 128], P('group')
Outputs:
- smoothed: float32 [16, 262144], P(None, ('group', 'fold'))
Inputs may be any that keep to these rules, and one draw needn't show every extreme that they name: Every row of counts sums to 8192, and its largest entry is 2048. `columns`: index j of row block g * 64 + i names block g * 64 + j - 3; the 5 indices of a row block are distinct and lie within 3 of i + 3.
All inputs are finite; a program needn't handle non-finite values.
Results may differ from a plain program's by a relative error of at most 0.0001.
Values sent between devices are 32-bit elements; how exact they have to be, the bound alone decides.
A program may use at most 192 MiB of HBM per device.

v0:
```python
import jax
import jax.numpy as jnp
from jax import lax
from jax.sharding import PartitionSpec as P

HB = 3
SWEEPS = 3
DEGREE = 4


upper_bound = 4.5
lower_bound = 1.35


def padded_2(shard, sides, width):
    for axis, dim in sides:
        devices, length = (lax.axis_size(axis), shard.shape[dim])
        up = [(i, (i + 1) % devices) for i in range(devices - 1)]
        down = [(j, i) for i, j in up]
        last = lax.slice_in_dim(shard, length - width, length, axis=dim)
        initial = lax.slice_in_dim(shard, 0, width, axis=dim)
        before = lax.ppermute(last, axis, up)
        after = lax.ppermute(initial, axis, down)
        shard = jnp.concatenate([before, shard, after], axis=dim)
    return shard


def on_device(right_side, initial, counts, columns, blocks):
    folds = lax.axis_size("fold")
    vectors, capacity = right_side.shape
    own_blocks, width = (blocks.shape[0], blocks.shape[2])
    live_rows = counts[0]
    starts = jnp.cumsum(live_rows) - live_rows
    stacked = jnp.stack([right_side, initial])
    gathered = lax.all_gather(stacked, "fold", axis=2, tiled=True)
    position = lax.axis_index("fold")
    row_ids = jnp.arange(own_blocks * width, dtype=jnp.int32)
    covered = starts[None, :] <= row_ids[:, None]
    owner_slot = jnp.sum(covered.astype(jnp.int32), axis=1) - 1
    row_start = jnp.max(jnp.where(covered, starts[None, :], 0), axis=1)
    source = owner_slot * capacity + row_ids - row_start
    owned = jnp.take(gathered, source, axis=2)
    target = owned[0]
    iterate = owned[1]

    def operate(vector):
        extended = padded_2(vector, (("group", 1),), HB * width)
        extended = extended.reshape(vectors, own_blocks + 2 * HB, width)
        picked = jnp.take(extended, columns, axis=1)
        result = jnp.einsum("nikc,ikrc->nir", picked, blocks, precision=lax.Precision.HIGHEST)
        return result.reshape(vectors, own_blocks * width)

    theta = (upper_bound + lower_bound) / 2.0
    delta = (upper_bound - lower_bound) / 2.0
    for sweep in range(SWEEPS):
        resid = target - operate(iterate)
        update = resid / theta
        ratio_now = delta / theta
        for step in range(DEGREE):
            iterate = iterate + update
            if step + 1 < DEGREE:
                resid = resid - operate(update)
                ratio_next = 1.0 / (2.0 * theta / delta - ratio_now)
                update = ratio_next * ratio_now * update + 2.0 * ratio_next / delta * resid
                ratio_now = ratio_next
    fold_ids = jnp.arange(folds, dtype=jnp.int32)
    my_start = jnp.sum(jnp.where(fold_ids == position, starts, 0))
    my_count = jnp.sum(jnp.where(fold_ids == position, live_rows, 0))
    padded = jnp.concatenate([iterate, jnp.zeros((vectors, capacity), jnp.float32)], axis=1)
    piece = lax.dynamic_slice_in_dim(padded, my_start, capacity, 1)
    valid = jnp.arange(capacity, dtype=jnp.int32) < my_count
    return jnp.where(valid[None, :], piece, jnp.float32(0.0))


def solution(mesh):
    placed = (
        P(None, ("group", "fold")),
        P(None, ("group", "fold")),
        P("group", None),
        P("group", None),
        P("group", None, None, None),
    )
    return jax.shard_map(
        on_device, mesh=mesh, in_specs=placed, out_specs=P(None, ("group", "fold")), check_vma=False
    )
```

profile of v0, /device:TPU:8, one launch (start us, length us, event | category | flops | bytes accessed | tf_op | source)
XLA Modules:
  0.0 559.3 jit_solution(11467768197865809706)
XLA Ops:
  11.8 24.7 %all-gather.2.cloned.1.call-done = f32[2,16,16384]{2,1,0:T(8,128)} async-done(((f32[2,16,2048]{2,1,0:T(8,128)}), f32[2,16,16384]{2,1,0:T(8,128)}) %all-gather.2.cloned.1.call-update) | async-done | bytes 2097168 | tf_op jit(solution)/shard_map/all_gather | solution.py:35
  36.5 18.6 %copy.304 = f32[2,16,16384]{1,0,2:T(2,128)} copy(f32[2,16,16384]{2,1,0:T(8,128)} %all-gather.2.cloned.1.call-done) | data formatting | bytes 4194304 | tf_op jit(solution)/shard_map/all_gather | solution.py:35
  55.2 62.3 %gather_fusion = f32[8192,2,16]{2,1,0:T(2,128)} fusion(f32[2,16,16384]{1,0,2:T(2,128)} %copy.304, s32[8192]{0:T(1024)S(1)} %broadcast_clamp_fusion), kind=kCustom, calls=%fused_computation.12 | custom fusion | bytes 2129920 | tf_op jit(solution)/shard_map/jit(_take)/gather | solution.py:42
  117.5 9.3 %copy.305 = f32[8192,2,16]{0,2,1:T(8,128)S(1)} copy(f32[8192,2,16]{2,1,0:T(2,128)} %gather_fusion) | data formatting | bytes 2097152 | tf_op jit(solution)/shard_map/jit(_take)/gather | solution.py:42
  127.0 3.4 collective-permute-start
  130.3 4.6 collective-permute-start.1
  136.5 1.9 gather_fusion.1
  138.4 23.1 %fusion.60 = f32[64,2,8,128]{3,2,1,0:T(8,128)S(1)} fusion(f32[64,5,128,128]{3,2,1,0:T(8,128)} %param.11, f32[64,5,16,128]{3,2,1,0:T(8,128)S(1)} %bitcast.334, pred[64,5]{1,0:T(8,128)(4,1)S(1)} %copy.306), kind=kOutput, calls=%fused_computation.73 | convolution fusion | flops 1007288320 | bytes 24117568 | tf_op jit(solution)/shard_map/nikc,ikrc->nir/dot_general | solution.py:50
  162.4 3.1 collective-permute-start.2
  165.5 5.4 collective-permute-start.3
  172.2 1.9 gather_fusion.2
  174.1 23.1 %fusion.63 = f32[64,2,8,128]{3,2,1,0:T(8,128)S(1)} fusion(f32[64,5,128,128]{3,2,1,0:T(8,128)} %param.11, f32[64,5,16,128]{3,2,1,0:T(8,128)S(1)} %bitcast.335, pred[64,5]{1,0:T(8,128)(4,1)S(1)} %copy.306), kind=kOutput, calls=%fused_computation.74 | convolution fusion | flops 1007288320 | bytes 24117568 | tf_op jit(solution)/shard_map/nikc,ikrc->nir/dot_general | solution.py:50
  197.4 3.6 collective-permute-start.4
  201.0 4.6 collective-permute-start.5
  207.2 1.9 gather_fusion.3
  209.1 23.1 %fusion.66 = f32[64,2,8,128]{3,2,1,0:T(8,128)S(1)} fusion(f32[64,5,128,128]{3,2,1,0:T(8,128)} %param.11, f32[64,5,16,128]{3,2,1,0:T(8,128)S(1)} %bitcast.336, pred[64,5]{1,0:T(8,128)(4,1)S(1)} %copy.306), kind=kOutput, calls=%fused_computation.75 | convolution fusion | flops 1007288320 | bytes 24117568 | tf_op jit(solution)/shard_map/nikc,ikrc->nir/dot_general | solution.py:50
  232.4 3.6 collective-permute-start.6
  236.0 5.2 collective-permute-start.7
  242.2 1.9 gather_fusion.4
  244.2 23.2 %fusion.69 = f32[64,2,8,128]{3,2,1,0:T(8,128)S(1)} fusion(f32[64,5,128,128]{3,2,1,0:T(8,128)} %param.11, f32[64,5,16,128]{3,2,1,0:T(8,128)S(1)} %bitcast.337, pred[64,5]{1,0:T(8,128)(4,1)S(1)} %copy.306), kind=kOutput, calls=%fused_computation.76 | convolution fusion | flops 1007288320 | bytes 24117568 | tf_op jit(solution)/shard_map/nikc,ikrc->nir/dot_general | solution.py:50
  267.7 3.6 collective-permute-start.8
  271.3 4.6 collective-permute-start.9
  277.5 1.9 gather_fusion.5
  279.4 23.1 %fusion.72 = f32[64,2,8,128]{3,2,1,0:T(8,128)S(1)} fusion(f32[64,5,128,128]{3,2,1,0:T(8,128)} %param.11, f32[64,5,16,128]{3,2,1,0:T(8,128)S(1)} %bitcast.338, pred[64,5]{1,0:T(8,128)(4,1)S(1)} %copy.306), kind=kOutput, calls=%fused_computation.77 | convolution fusion | flops 1007288320 | bytes 24117568 | tf_op jit(solution)/shard_map/nikc,ikrc->nir/dot_general | solution.py:50
  303.4 3.6 collective-permute-start.10
  307.0 4.8 collective-permute-start.11
  313.2 1.9 gather_fusion.6
  315.1 23.1 %fusion.75 = f32[64,2,8,128]{3,2,1,0:T(8,128)S(1)} fusion(f32[64,5,128,128]{3,2,1,0:T(8,128)} %param.11, f32[64,5,16,128]{3,2,1,0:T(8,128)S(1)} %bitcast.339, pred[64,5]{1,0:T(8,128)(4,1)S(1)} %copy.306), kind=kOutput, calls=%fused_computation.78 | convolution fusion | flops 1007288320 | bytes 24117568 | tf_op jit(solution)/shard_map/nikc,ikrc->nir/dot_general | solution.py:50
  338.4 3.6 collective-permute-start.12
  342.0 4.6 collective-permute-start.13
  348.2 1.9 gather_fusion.7
  350.1 23.1 %fusion.78 = f32[64,2,8,128]{3,2,1,0:T(8,128)S(1)} fusion(f32[64,5,128,128]{3,2,1,0:T(8,128)} %param.11, f32[64,5,16,128]{3,2,1,0:T(8,128)S(1)} %bitcast.340, pred[64,5]{1,0:T(8,128)(4,1)S(1)} %copy.306), kind=kOutput, calls=%fused_computation.79 | convolution fusion | flops 1007288320 | bytes 24117568 | tf_op jit(solution)/shard_map/nikc,ikrc->nir/dot_general | solution.py:50
  373.4 3.6 collective-permute-start.14
  377.0 4.9 collective-permute-start.15
  385.2 23.2 %fusion.81 = f32[64,2,8,128]{3,2,1,0:T(8,128)S(1)} fusion(f32[64,5,128,128]{3,2,1,0:T(8,128)} %param.11, f32[64,5,16,128]{3,2,1,0:T(8,128)S(1)} %bitcast.341, pred[64,5]{1,0:T(8,128)(4,1)S(1)} %copy.306), kind=kOutput, calls=%fused_computation.80 | convolution fusion | flops 1007288320 | bytes 24117568 | tf_op jit(solution)/shard_map/nikc,ikrc->nir/dot_general | solution.py:50
  408.7 3.6 collective-permute-start.16
  412.3 4.6 collective-permute-start.17
  420.4 23.1 %fusion.84 = f32[64,2,8,128]{3,2,1,0:T(8,128)S(1)} fusion(f32[64,5,128,128]{3,2,1,0:T(8,128)} %param.11, f32[64,5,16,128]{3,2,1,0:T(8,128)S(1)} %bitcast.342, pred[64,5]{1,0:T(8,128)(4,1)S(1)} %copy.306), kind=kOutput, calls=%fused_computation.81 | convolution fusion | flops 1007288320 | bytes 24117568 | tf_op jit(solution)/shard_map/nikc,ikrc->nir/dot_general | solution.py:50
  444.5 3.6 collective-permute-start.18
  448.1 5.0 collective-permute-start.19
  454.3 1.9 gather_fusion.10
  456.2 23.1 %fusion.87 = f32[64,2,8,128]{3,2,1,0:T(8,128)S(1)} fusion(f32[64,5,128,128]{3,2,1,0:T(8,128)} %param.11, f32[64,5,16,128]{3,2,1,0:T(8,128)S(1)} %bitcast.343, pred[64,5]{1,0:T(8,128)(4,1)S(1)} %copy.306), kind=kOutput, calls=%fused_computation.82 | convolution fusion | flops 1007288320 | bytes 24117568 | tf_op jit(solution)/shard_map/nikc,ikrc->nir/dot_general | solution.py:50
  479.4 3.6 collective-permute-start.20
  483.0 4.6 collective-permute-start.21
  491.2 23.1 %fusion.90 = f32[64,2,8,128]{3,2,1,0:T(8,128)S(1)} fusion(f32[64,5,128,128]{3,2,1,0:T(8,128)} %param.11, f32[64,5,16,128]{3,2,1,0:T(8,128)S(1)} %bitcast.344, pred[64,5]{1,0:T(8,128)(4,1)S(1)} %copy.306), kind=kOutput, calls=%fused_computation.83 | convolution fusion | flops 1007288320 | bytes 24117568 | tf_op jit(solution)/shard_map/nikc,ikrc->nir/dot_general | solution.py:50
  515.2 3.6 collective-permute-start.22
  518.8 4.8 collective-permute-start.23
  528.0 23.2 %fusion.93 = f32[64,2,8,128]{3,2,1,0:T(8,128)S(1)} fusion(f32[64,5,128,128]{3,2,1,0:T(8,128)} %param.11, f32[64,5,16,128]{3,2,1,0:T(8,128)S(1)} %bitcast.333, pred[64,5]{1,0:T(8,128)(4,1)S(1)} %copy.306), kind=kOutput, calls=%fused_computation.84 | convolution fusion | flops 1007288320 | bytes 24117568 | tf_op jit(solution)/shard_map/nikc,ikrc->nir/dot_general | solution.py:50
  (175 shorter events, 34.8 us)
Async XLA Ops:
  6.5 30.0 %all-gather.2.cloned.1.call-start = ((), (), s32[]{:S(2)}) async-start(), calls=%async_computation | async-start | bytes 2359296 | tf_op jit(solution)/shard_map/all_gather | solution.py:35
  127.0 8.1 %collective-permute-start = (f32[16,384]{1,0:T(8,128)S(1)}, f32[16,384]{1,0:T(8,128)S(1)}, u32[]{:S(2)}, u32[]{:S(2)}) collective-permute-start(f32[16,384]{1,0:T(8,128)S(1)} %get-tuple-element.38), channel_id=1, source_target_pairs={{0,8},{8,16},{16,24},{24,32},{32,40},{40,48},{48,56},{56,64},{64,7... | collective-permute-start | bytes 73736 | tf_op jit(solution)/shard_map/ppermute | solution.py:22
  130.3 6.1 %collective-permute-start.1 = (f32[16,384]{1,0:T(8,128)S(1)}, f32[16,384]{1,0:T(8,128)S(1)}, u32[]{:S(2)}, u32[]{:S(2)}) collective-permute-start(f32[16,384]{1,0:T(8,128)S(1)} %get-tuple-element.39), channel_id=1, source_target_pairs={{8,0},{16,8},{24,16},{32,24},{40,32},{48,40},{56,48},{64,56},{72,6... | collective-permute-start | bytes 73736 | tf_op jit(solution)/shard_map/ppermute | solution.py:23
  162.4 8.5 %collective-permute-start.2 = (f32[16,384]{1,0:T(8,128)S(1)}, f32[16,384]{1,0:T(8,128)S(1)}, u32[]{:S(2)}, u32[]{:S(2)}) collective-permute-start(f32[16,384]{1,0:T(8,128)S(1)} %get-tuple-element.36), channel_id=1, source_target_pairs={{0,8},{8,16},{16,24},{24,32},{32,40},{40,48},{48,56},{56,64},{64,7... | collective-permute-start | bytes 73736 | tf_op jit(solution)/shard_map/ppermute | solution.py:22
  165.5 6.7 %collective-permute-start.3 = (f32[16,384]{1,0:T(8,128)S(1)}, f32[16,384]{1,0:T(8,128)S(1)}, u32[]{:S(2)}, u32[]{:S(2)}) collective-permute-start(f32[16,384]{1,0:T(8,128)S(1)} %get-tuple-element.37), channel_id=1, source_target_pairs={{8,0},{16,8},{24,16},{32,24},{40,32},{48,40},{56,48},{64,56},{72,6... | collective-permute-start | bytes 73736 | tf_op jit(solution)/shard_map/ppermute | solution.py:23
  197.4 8.3 %collective-permute-start.4 = (f32[16,384]{1,0:T(8,128)S(1)}, f32[16,384]{1,0:T(8,128)S(1)}, u32[]{:S(2)}, u32[]{:S(2)}) collective-permute-start(f32[16,384]{1,0:T(8,128)S(1)} %get-tuple-element.34), channel_id=1, source_target_pairs={{0,8},{8,16},{16,24},{24,32},{32,40},{40,48},{48,56},{56,64},{64,7... | collective-permute-start | bytes 73736 | tf_op jit(solution)/shard_map/ppermute | solution.py:22
  201.0 6.1 %collective-permute-start.5 = (f32[16,384]{1,0:T(8,128)S(1)}, f32[16,384]{1,0:T(8,128)S(1)}, u32[]{:S(2)}, u32[]{:S(2)}) collective-permute-start(f32[16,384]{1,0:T(8,128)S(1)} %get-tuple-element.35), channel_id=1, source_target_pairs={{8,0},{16,8},{24,16},{32,24},{40,32},{48,40},{56,48},{64,56},{72,6... | collective-permute-start | bytes 73736 | tf_op jit(solution)/shard_map/ppermute | solution.py:23
  209.1 23.2 %copy-start.21 = (f32[16,8192]{1,0:T(8,128)S(1)}, f32[16,8192]{1,0:T(8,128)}, u32[]{:S(2)}) copy-start(f32[16,8192]{1,0:T(8,128)} %copy-done.20) | copy-start | bytes 1572868
  209.1 23.2 %copy-start.30 = (f32[16,8192]{1,0:T(8,128)S(1)}, f32[16,8192]{1,0:T(8,128)}, u32[]{:S(2)}) copy-start(f32[16,8192]{1,0:T(8,128)} %get-tuple-element.15) | copy-start | bytes 1572868
  232.4 8.8 %collective-permute-start.6 = (f32[16,384]{1,0:T(8,128)S(1)}, f32[16,384]{1,0:T(8,128)S(1)}, u32[]{:S(2)}, u32[]{:S(2)}) collective-permute-start(f32[16,384]{1,0:T(8,128)S(1)} %get-tuple-element.32), channel_id=1, source_target_pairs={{0,8},{8,16},{16,24},{24,32},{32,40},{40,48},{48,56},{56,64},{64,7... | collective-permute-start | bytes 73736 | tf_op jit(solution)/shard_map/ppermute | solution.py:22
  236.0 6.1 %collective-permute-start.7 = (f32[16,384]{1,0:T(8,128)S(1)}, f32[16,384]{1,0:T(8,128)S(1)}, u32[]{:S(2)}, u32[]{:S(2)}) collective-permute-start(f32[16,384]{1,0:T(8,128)S(1)} %get-tuple-element.33), channel_id=1, source_target_pairs={{8,0},{16,8},{24,16},{32,24},{40,32},{48,40},{56,48},{64,56},{72,6... | collective-permute-start | bytes 73736 | tf_op jit(solution)/shard_map/ppermute | solution.py:23
  244.1 23.2 %copy-start.2 = (f32[2,16,8192]{2,1,0:T(8,128)S(1)}, f32[2,16,8192]{2,1,0:T(8,128)}, u32[]{:S(2)}) copy-start(f32[2,16,8192]{2,1,0:T(8,128)} %copy-done) | copy-start | bytes 3145732
  244.1 23.2 %copy-start.13 = (f32[64,2,8,128]{3,2,1,0:T(8,128)S(1)}, f32[64,2,8,128]{3,2,1,0:T(8,128)}, u32[]{:S(2)}) copy-start(f32[64,2,8,128]{3,2,1,0:T(8,128)} %copy-done.11) | copy-start | bytes 1572868
  244.2 23.2 %copy-start.22 = (f32[16,8192]{1,0:T(8,128)S(1)}, f32[16,8192]{1,0:T(8,128)}, u32[]{:S(2)}) copy-start(f32[16,8192]{1,0:T(8,128)} %copy-done.20) | copy-start | bytes 1572868
  244.2 23.2 %copy-start.31 = (f32[16,8192]{1,0:T(8,128)S(1)}, f32[16,8192]{1,0:T(8,128)}, u32[]{:S(2)}) copy-start(f32[16,8192]{1,0:T(8,128)} %get-tuple-element.15) | copy-start | bytes 1572868
  244.2 23.2 %copy-start.37 = (f32[64,2,8,128]{3,2,1,0:T(8,128)S(1)}, f32[64,2,8,128]{3,2,1,0:T(8,128)}, u32[]{:S(2)}) copy-start(f32[64,2,8,128]{3,2,1,0:T(8,128)} %copy-done.36) | copy-start | bytes 1572868
  267.7 8.3 %collective-permute-start.8 = (f32[16,384]{1,0:T(8,128)S(1)}, f32[16,384]{1,0:T(8,128)S(1)}, u32[]{:S(2)}, u32[]{:S(2)}) collective-permute-start(f32[16,384]{1,0:T(8,128)S(1)} %get-tuple-element.30), channel_id=1, source_target_pairs={{0,8},{8,16},{16,24},{24,32},{32,40},{40,48},{48,56},{56,64},{64,7... | collective-permute-start | bytes 73736 | tf_op jit(solution)/shard_map/ppermute | solution.py:22
  271.3 6.1 %collective-permute-start.9 = (f32[16,384]{1,0:T(8,128)S(1)}, f32[16,384]{1,0:T(8,128)S(1)}, u32[]{:S(2)}, u32[]{:S(2)}) collective-permute-start(f32[16,384]{1,0:T(8,128)S(1)} %get-tuple-element.31), channel_id=1, source_target_pairs={{8,0},{16,8},{24,16},{32,24},{40,32},{48,40},{56,48},{64,56},{72,6... | collective-permute-start | bytes 73736 | tf_op jit(solution)/shard_map/ppermute | solution.py:23
  303.4 8.4 %collective-permute-start.10 = (f32[16,384]{1,0:T(8,128)S(1)}, f32[16,384]{1,0:T(8,128)S(1)}, u32[]{:S(2)}, u32[]{:S(2)}) collective-permute-start(f32[16,384]{1,0:T(8,128)S(1)} %get-tuple-element.28), channel_id=1, source_target_pairs={{0,8},{8,16},{16,24},{24,32},{32,40},{40,48},{48,56},{56,64},{64,7... | collective-permute-start | bytes 73736 | tf_op jit(solution)/shard_map/ppermute | solution.py:22
  307.0 6.1 %collective-permute-start.11 = (f32[16,384]{1,0:T(8,128)S(1)}, f32[16,384]{1,0:T(8,128)S(1)}, u32[]{:S(2)}, u32[]{:S(2)}) collective-permute-start(f32[16,384]{1,0:T(8,128)S(1)} %get-tuple-element.29), channel_id=1, source_target_pairs={{8,0},{16,8},{24,16},{32,24},{40,32},{48,40},{56,48},{64,56},{72,6... | collective-permute-start | bytes 73736 | tf_op jit(solution)/shard_map/ppermute | solution.py:23
  338.4 8.3 %collective-permute-start.12 = (f32[16,384]{1,0:T(8,128)S(1)}, f32[16,384]{1,0:T(8,128)S(1)}, u32[]{:S(2)}, u32[]{:S(2)}) collective-permute-start(f32[16,384]{1,0:T(8,128)S(1)} %get-tuple-element.26), channel_id=1, source_target_pairs={{0,8},{8,16},{16,24},{24,32},{32,40},{40,48},{48,56},{56,64},{64,7... | collective-permute-start | bytes 73736 | tf_op jit(solution)/shard_map/ppermute | solution.py:22
  342.0 6.1 %collective-permute-start.13 = (f32[16,384]{1,0:T(8,128)S(1)}, f32[16,384]{1,0:T(8,128)S(1)}, u32[]{:S(2)}, u32[]{:S(2)}) collective-permute-start(f32[16,384]{1,0:T(8,128)S(1)} %get-tuple-element.27), channel_id=1, source_target_pairs={{8,0},{16,8},{24,16},{32,24},{40,32},{48,40},{56,48},{64,56},{72,6... | collective-permute-start | bytes 73736 | tf_op jit(solution)/shard_map/ppermute | solution.py:23
  350.1 23.2 %copy-start.18 = (f32[16,8192]{1,0:T(8,128)S(1)}, f32[16,8192]{1,0:T(8,128)}, u32[]{:S(2)}) copy-start(f32[16,8192]{1,0:T(8,128)} %copy-done.17) | copy-start | bytes 1572868
  350.1 23.2 %copy-start.27 = (f32[16,8192]{1,0:T(8,128)S(1)}, f32[16,8192]{1,0:T(8,128)}, u32[]{:S(2)}) copy-start(f32[16,8192]{1,0:T(8,128)} %get-tuple-element.13) | copy-start | bytes 1572868
  373.4 8.5 %collective-permute-start.14 = (f32[16,384]{1,0:T(8,128)S(1)}, f32[16,384]{1,0:T(8,128)S(1)}, u32[]{:S(2)}, u32[]{:S(2)}) collective-permute-start(f32[16,384]{1,0:T(8,128)S(1)} %get-tuple-element.24), channel_id=1, source_target_pairs={{0,8},{8,16},{16,24},{24,32},{32,40},{40,48},{48,56},{56,64},{64,7... | collective-permute-start | bytes 73736 | tf_op jit(solution)/shard_map/ppermute | solution.py:22
  377.0 6.1 %collective-permute-start.15 = (f32[16,384]{1,0:T(8,128)S(1)}, f32[16,384]{1,0:T(8,128)S(1)}, u32[]{:S(2)}, u32[]{:S(2)}) collective-permute-start(f32[16,384]{1,0:T(8,128)S(1)} %get-tuple-element.25), channel_id=1, source_target_pairs={{8,0},{16,8},{24,16},{32,24},{40,32},{48,40},{56,48},{64,56},{72,6... | collective-permute-start | bytes 73736 | tf_op jit(solution)/shard_map/ppermute | solution.py:23
  385.1 23.2 %copy-start.10 = (f32[64,2,8,128]{3,2,1,0:T(8,128)S(1)}, f32[64,2,8,128]{3,2,1,0:T(8,128)}, u32[]{:S(2)}) copy-start(f32[64,2,8,128]{3,2,1,0:T(8,128)} %copy-done.8) | copy-start | bytes 1572868
  385.1 23.2 %copy-start.19 = (f32[16,8192]{1,0:T(8,128)S(1)}, f32[16,8192]{1,0:T(8,128)}, u32[]{:S(2)}) copy-start(f32[16,8192]{1,0:T(8,128)} %copy-done.17) | copy-start | bytes 1572868
  385.2 23.2 %copy-start.28 = (f32[16,8192]{1,0:T(8,128)S(1)}, f32[16,8192]{1,0:T(8,128)}, u32[]{:S(2)}) copy-start(f32[16,8192]{1,0:T(8,128)} %get-tuple-element.13) | copy-start | bytes 1572868
  385.2 23.2 %copy-start.35 = (f32[64,2,8,128]{3,2,1,0:T(8,128)S(1)}, f32[64,2,8,128]{3,2,1,0:T(8,128)}, u32[]{:S(2)}) copy-start(f32[64,2,8,128]{3,2,1,0:T(8,128)} %copy-done.34) | copy-start | bytes 1572868
  385.2 23.2 %copy-start.41 = (f32[16,8192]{1,0:T(8,128)S(1)}, f32[16,8192]{1,0:T(8,128)}, u32[]{:S(2)}) copy-start(f32[16,8192]{1,0:T(8,128)} %copy-done.40) | copy-start | bytes 1572868
  408.7 8.3 %collective-permute-start.16 = (f32[16,384]{1,0:T(8,128)S(1)}, f32[16,384]{1,0:T(8,128)S(1)}, u32[]{:S(2)}, u32[]{:S(2)}) collective-permute-start(f32[16,384]{1,0:T(8,128)S(1)} %get-tuple-element.22), channel_id=1, source_target_pairs={{0,8},{8,16},{16,24},{24,32},{32,40},{40,48},{48,56},{56,64},{64,7... | collective-permute-start | bytes 73736 | tf_op jit(solution)/shard_map/ppermute | solution.py:22
  412.3 6.1 %collective-permute-start.17 = (f32[16,384]{1,0:T(8,128)S(1)}, f32[16,384]{1,0:T(8,128)S(1)}, u32[]{:S(2)}, u32[]{:S(2)}) collective-permute-start(f32[16,384]{1,0:T(8,128)S(1)} %get-tuple-element.23), channel_id=1, source_target_pairs={{8,0},{16,8},{24,16},{32,24},{40,32},{48,40},{56,48},{64,56},{72,6... | collective-permute-start | bytes 73736 | tf_op jit(solution)/shard_map/ppermute | solution.py:23
  444.5 8.7 %collective-permute-start.18 = (f32[16,384]{1,0:T(8,128)S(1)}, f32[16,384]{1,0:T(8,128)S(1)}, u32[]{:S(2)}, u32[]{:S(2)}) collective-permute-start(f32[16,384]{1,0:T(8,128)S(1)} %get-tuple-element.20), channel_id=1, source_target_pairs={{0,8},{8,16},{16,24},{24,32},{32,40},{40,48},{48,56},{56,64},{64,7... | collective-permute-start | bytes 73736 | tf_op jit(solution)/shard_map/ppermute | solution.py:22
  448.1 6.1 %collective-permute-start.19 = (f32[16,384]{1,0:T(8,128)S(1)}, f32[16,384]{1,0:T(8,128)S(1)}, u32[]{:S(2)}, u32[]{:S(2)}) collective-permute-start(f32[16,384]{1,0:T(8,128)S(1)} %get-tuple-element.21), channel_id=1, source_target_pairs={{8,0},{16,8},{24,16},{32,24},{40,32},{48,40},{56,48},{64,56},{72,6... | collective-permute-start | bytes 73736 | tf_op jit(solution)/shard_map/ppermute | solution.py:23
  456.2 31.5 %copy-start.42 = (s32[1,8]{1,0:T(1,128)S(1)}, s32[1,8]{1,0:T(1,128)}, u32[]{:S(2)}) copy-start(s32[1,8]{1,0:T(1,128)} %param.9) | copy-start | bytes 100
  456.2 31.5 %copy-start.44 = (s32[8,1]{0,1:T(1,128)S(1)}, s32[8,1]{0,1:T(1,128)}, u32[]{:S(2)}) copy-start(s32[8,1]{0,1:T(1,128)} %copy-done.43) | copy-start | bytes 100
  479.4 8.9 %collective-permute-start.20 = (f32[16,384]{1,0:T(8,128)S(1)}, f32[16,384]{1,0:T(8,128)S(1)}, u32[]{:S(2)}, u32[]{:S(2)}) collective-permute-start(f32[16,384]{1,0:T(8,128)S(1)} %get-tuple-element.18), channel_id=1, source_target_pairs={{0,8},{8,16},{16,24},{24,32},{32,40},{40,48},{48,56},{56,64},{64,7... | collective-permute-start | bytes 73736 | tf_op jit(solution)/shard_map/ppermute | solution.py:22
  483.0 6.1 %collective-permute-start.21 = (f32[16,384]{1,0:T(8,128)S(1)}, f32[16,384]{1,0:T(8,128)S(1)}, u32[]{:S(2)}, u32[]{:S(2)}) collective-permute-start(f32[16,384]{1,0:T(8,128)S(1)} %get-tuple-element.19), channel_id=1, source_target_pairs={{8,0},{16,8},{24,16},{32,24},{40,32},{48,40},{56,48},{64,56},{72,6... | collective-permute-start | bytes 73736 | tf_op jit(solution)/shard_map/ppermute | solution.py:23
  491.2 23.2 %copy-start.15 = (f32[16,8192]{1,0:T(8,128)S(1)}, f32[16,8192]{1,0:T(8,128)}, u32[]{:S(2)}) copy-start(f32[16,8192]{1,0:T(8,128)} %copy-done.14) | copy-start | bytes 1572868
  491.2 23.2 %copy-start.24 = (f32[16,8192]{1,0:T(8,128)S(1)}, f32[16,8192]{1,0:T(8,128)}, u32[]{:S(2)}) copy-start(f32[16,8192]{1,0:T(8,128)} %get-tuple-element.11) | copy-start | bytes 1572868
  515.2 10.8 %collective-permute-start.22 = (f32[16,384]{1,0:T(8,128)S(1)}, f32[16,384]{1,0:T(8,128)S(1)}, u32[]{:S(2)}, u32[]{:S(2)}) collective-permute-start(f32[16,384]{1,0:T(8,128)S(1)} %get-tuple-element.16), channel_id=1, source_target_pairs={{0,8},{8,16},{16,24},{24,32},{32,40},{40,48},{48,56},{56,64},{64,7... | collective-permute-start | bytes 73736 | tf_op jit(solution)/shard_map/ppermute | solution.py:22
  518.8 7.2 %collective-permute-start.23 = (f32[16,384]{1,0:T(8,128)S(1)}, f32[16,384]{1,0:T(8,128)S(1)}, u32[]{:S(2)}, u32[]{:S(2)}) collective-permute-start(f32[16,384]{1,0:T(8,128)S(1)} %get-tuple-element.17), channel_id=1, source_target_pairs={{8,0},{16,8},{24,16},{32,24},{40,32},{48,40},{56,48},{64,56},{72,6... | collective-permute-start | bytes 73736 | tf_op jit(solution)/shard_map/ppermute | solution.py:23
  527.9 23.2 %copy-start.7 = (f32[64,2,8,128]{3,2,1,0:T(8,128)S(1)}, f32[64,2,8,128]{3,2,1,0:T(8,128)}, u32[]{:S(2)}) copy-start(f32[64,2,8,128]{3,2,1,0:T(8,128)} %copy-done.5) | copy-start | bytes 1572868
  527.9 23.2 %copy-start.16 = (f32[16,8192]{1,0:T(8,128)S(1)}, f32[16,8192]{1,0:T(8,128)}, u32[]{:S(2)}) copy-start(f32[16,8192]{1,0:T(8,128)} %copy-done.14) | copy-start | bytes 1572868
  528.0 23.2 %copy-start.25 = (f32[16,8192]{1,0:T(8,128)S(1)}, f32[16,8192]{1,0:T(8,128)}, u32[]{:S(2)}) copy-start(f32[16,8192]{1,0:T(8,128)} %get-tuple-element.11) | copy-start | bytes 1572868
  528.0 23.2 %copy-start.33 = (f32[64,2,8,128]{3,2,1,0:T(8,128)S(1)}, f32[64,2,8,128]{3,2,1,0:T(8,128)}, u32[]{:S(2)}) copy-start(f32[64,2,8,128]{3,2,1,0:T(8,128)} %copy-done.32) | copy-start | bytes 1572868
  528.0 23.2 %copy-start.39 = (f32[16,8192]{1,0:T(8,128)S(1)}, f32[16,8192]{1,0:T(8,128)}, u32[]{:S(2)}) copy-start(f32[16,8192]{1,0:T(8,128)} %copy-done.38) | copy-start | bytes 1572868
  (22 other events, 312.6 us)
Sparse Core Ops, SparseCore 0:
  9.0 27.4 all-gather.1
where the time goes:
time: 567 us; the launch traced here: 559 us
  matrix products  277 us (49%)
  local copies, waits for them, and re-layouts  115 us (20%)
  starting transfers between devices  100 us (18%)
  waiting for transfers between devices  38.7 us (7%)
  between operations  16.6 us (3%)
  other arithmetic  11.6 us (2%)
    dot_general x12, matrix products, operate(): jnp.einsum('nikc,ikrc->nir', picked, blocks, precision=lax.Precision.HIGH...  277 us
    gather x2, local copies, waits for them, and re-layouts, on_device(): owned = jnp.take(gathered, source, axis=2)  71.6 us
    ppermute x12, starting transfers between devices, padded_2(): after = lax.ppermute(initial, axis, down)  57.9 us
    ppermute x12, starting transfers between devices, padded_2(): before = lax.ppermute(last, axis, up)  42.5 us
    all_gather x1, waiting for transfers between devices, on_device(): gathered = lax.all_gather(stacked, 'fold', axis=2, tiled=True)  24.7 us
    gather x12, local copies, waits for them, and re-layouts, operate(): picked = jnp.take(extended, columns, axis=1)  22.7 us
    all_gather x1, local copies, waits for them, and re-layouts, on_device(): gathered = lax.all_gather(stacked, 'fold', axis=2, tiled=True)  18.6 us
    ppermute x12, waiting for transfers between devices, padded_2(): after = lax.ppermute(initial, axis, down)  14 us
  transfers between devices with their start and end apart: 25, of which 12 were waited for; matrix products, arithmetic and copies ran while one was open for 1% of the time, Pallas kernels for 0%

commit v1 on v0

v1 whole, which is shorter than its diff:
```python
import functools

import jax
import jax.numpy as jnp
import numpy as np
from jax import lax
from jax.experimental import pallas as pl
from jax.experimental.pallas import tpu as pltpu
from jax.sharding import PartitionSpec as P

MESH = pl.DeviceIdType.MESH
HB = 3
SWEEPS = 3
DEGREE = 4
KB = 5
NV = 16
LANES = 128
FOLDS = 8
CHIPS = 4

upper_bound = 4.5
lower_bound = 1.35


def step_factors():
    theta = (upper_bound + lower_bound) / 2.0
    delta = (upper_bound - lower_bound) / 2.0
    keep, gain = [0.0], [1.0 / theta]
    for sweep in range(SWEEPS):
        ratio = delta / theta
        for step in range(DEGREE - 1):
            ratio_next = 1.0 / (2.0 * theta / delta - ratio)
            keep.append(ratio_next * ratio)
            gain.append(2.0 * ratio_next / delta)
            ratio = ratio_next
        if sweep + 1 < SWEEPS:
            keep.append(0.0)
            gain.append(1.0 / theta)
    return np.array([keep, gain], np.float32)


def split(value):
    high = value.astype(jnp.bfloat16)
    low = (value - high.astype(jnp.float32)).astype(jnp.bfloat16)
    return high, low


def position_of(fold):
    chip, core = fold // 2, fold % 2
    return chip + core * (7 - 2 * chip)


def fold_of(position):
    core = position // 4
    chip = position + core * (7 - 2 * position)
    return 2 * chip + core


def kernel(
    steps, rows, groups,
    factors, counts, columns, right_side, initial, blocks, out,
    raw, aligned, sent, parts, raw_blocks, weights, order, vector, update, resid, iterate, partial, halo, gathered,
    block_sem, a_send, a_recv, b_send, b_recv, h_send, h_recv, c_send, c_recv,
):
    group, fold = lax.axis_index("group"), lax.axis_index("fold")
    chip, core = fold // 2, fold % 2
    place = position_of(fold)
    partner = chip * 2 + (1 - core)
    slots = right_side.shape[1] // LANES
    total_rows = rows * FOLDS

    own_blocks = pltpu.make_async_copy(blocks.at[pl.ds(place * rows, rows)], raw_blocks, block_sem)
    own_blocks.start()

    rank = group * FOLDS + place
    has_left, has_right = rank > 0, rank < groups * FOLDS - 1
    at_left, at_right = place == 0, place == FOLDS - 1
    left = {"group": group - (7 - place) // 7, "fold": fold_of((place + 7) % 8)}
    right = {"group": group + place // 7, "fold": fold_of((place + 1) % 8)}

    barrier = pltpu.get_barrier_semaphore()
    for other in range(1, FOLDS):
        pl.semaphore_signal(barrier, inc=1, device_id={"group": group, "fold": (fold + other) % FOLDS}, device_id_type=MESH)

    @pl.when(jnp.logical_and(at_left, has_left))
    def _():
        pl.semaphore_signal(barrier, inc=1, device_id=left, device_id_type=MESH)

    @pl.when(jnp.logical_and(at_right, has_right))
    def _():
        pl.semaphore_signal(barrier, inc=1, device_id=right, device_id_type=MESH)

    last = groups * FOLDS - 1
    outside = (7 - place) // 7 * ((rank + last) // (last + 1)) + place // 7 * (1 - (rank + 1) // (last + 1))
    pl.semaphore_wait(barrier, FOLDS - 1 + outside)

    def swap(source):
        return pltpu.make_async_remote_copy(
            src_ref=source, dst_ref=raw, send_sem=a_send, recv_sem=a_recv,
            device_id={"group": group, "fold": partner}, device_id_type=MESH,
        )

    @pl.when(core == 0)
    def _():
        swap(initial).start()

    @pl.when(core == 1)
    def _():
        swap(right_side).start()

    lane = lax.broadcasted_iota(jnp.int32, (NV, LANES), 1)

    def start_of(which):
        total = jnp.int32(0)
        for i in range(FOLDS):
            total = total + jnp.where(i < which, counts[0, i], 0)
        return total

    def count_of(which):
        total = jnp.int32(0)
        for i in range(FOLDS):
            total = total + jnp.where(i == which, counts[0, i], 0)
        return total

    def align(source, which):
        start, count = start_of(chip * 2 + which), count_of(chip * 2 + which)
        shift = start & (LANES - 1)
        aligned[which, 0] = jnp.zeros((NV, LANES), jnp.float32)
        aligned[which, slots + 2] = jnp.zeros((NV, LANES), jnp.float32)
        before = jnp.zeros((NV, LANES), jnp.float32)
        for m in range(slots + 1):
            if m < slots:
                now = pltpu.roll(source[:, m * LANES:(m + 1) * LANES], shift, 1)
            else:
                now = jnp.zeros((NV, LANES), jnp.float32)
            slot = lane + (m * LANES - shift)
            value = jnp.where(lane < shift, before, now)
            live = jnp.logical_and(slot >= 0, slot < count)
            aligned[which, m + 1] = jnp.where(live, value, 0.0)
            before = now

    @pl.when(core == 0)
    def _():
        align(right_side, 0)

    @pl.when(core == 1)
    def _():
        align(initial, 1)

    swap(initial).wait()

    @pl.when(core == 0)
    def _():
        align(raw, 1)

    @pl.when(core == 1)
    def _():
        align(raw, 0)

    first = [start_of(chip * 2) // LANES, start_of(chip * 2 + 1) // LANES]

    def row_block(index):
        at = [jnp.clip(index - first[i], -1, slots + 1) + 1 for i in range(2)]
        return aligned[0, at[0]] + aligned[1, at[1]]

    def message(other):
        dest = (fold + other) % FOLDS
        where = position_of(dest) * rows
        return where, pltpu.make_async_remote_copy(
            src_ref=sent.at[pl.ds(where, rows)], dst_ref=parts.at[fold],
            send_sem=b_send.at[other], recv_sem=b_recv.at[fold],
            device_id={"group": group, "fold": dest}, device_id_type=MESH,
        )

    def arrival(source):
        return pltpu.make_async_remote_copy(
            src_ref=sent.at[pl.ds(0, rows)], dst_ref=parts.at[source],
            send_sem=b_send.at[0], recv_sem=b_recv.at[source],
            device_id={"group": group, "fold": fold}, device_id_type=MESH,
        )

    for other in (4, 3, 5, 2, 6, 1, 7):
        where, copy = message(other)
        for b in range(rows):
            sent[where + b] = row_block(where + b)
        copy.start()
    for b in range(rows):
        parts[fold, b] = row_block(place * rows + b)

    own_blocks.wait()
    zero = jnp.zeros((NV, LANES), jnp.float32)

    @pl.loop(0, rows)
    def _(j):
        column = [columns[place * rows + j, k] for k in range(KB)]
        ranks = []
        for k in range(KB):
            r = jnp.int32(0)
            for other in range(KB):
                if other != k:
                    ahead = column[other] <= column[k] if other < k else column[other] < column[k]
                    r = r + ahead.astype(jnp.int32)
            ranks.append(r)
        for s in range(KB):
            from_slot, at = jnp.int32(0), jnp.int32(0)
            for k in range(KB):
                from_slot = from_slot + jnp.where(ranks[k] == s, k, 0)
                at = at + jnp.where(ranks[k] == s, column[k], 0)
            order[j, s] = jnp.clip(at - place * rows, 0, rows + 2 * HB - 1)
            high, low = split(raw_blocks[j, from_slot].T)
            weights[j, s * LANES:(s + 1) * LANES, 0:LANES] = high
            weights[j, s * LANES:(s + 1) * LANES, LANES:2 * LANES] = low
        iterate[j] = zero

    @pl.when(jnp.logical_not(has_left))
    def _():
        for parity in range(2):
            for b in range(HB):
                halo[parity, 0, b] = zero

    @pl.when(jnp.logical_not(has_right))
    def _():
        for parity in range(2):
            for b in range(HB):
                halo[parity, 1, b] = zero

    for other in range(1, FOLDS):
        arrival((fold + other) % FOLDS).wait_recv()
    for b in range(rows):
        resid[b] = (parts[0, b] + parts[2, b]) + (parts[4, b] + parts[6, b])
        update[0, b] = (parts[1, b] + parts[3, b]) + (parts[5, b] + parts[7, b])
    for other in range(1, FOLDS):
        message(other)[1].wait_send()

    def to_left(parity):
        return pltpu.make_async_remote_copy(
            src_ref=update.at[parity, pl.ds(0, HB)], dst_ref=halo.at[parity, 1],
            send_sem=h_send.at[parity, 0], recv_sem=h_recv.at[parity, 1],
            device_id=left, device_id_type=MESH,
        )

    def to_right(parity):
        return pltpu.make_async_remote_copy(
            src_ref=update.at[parity, pl.ds(rows - HB, HB)], dst_ref=halo.at[parity, 0],
            send_sem=h_send.at[parity, 1], recv_sem=h_recv.at[parity, 0],
            device_id=right, device_id_type=MESH,
        )

    def store_vector(index, value):
        high, low = split(value)
        vector[index, 0:NV] = high
        vector[index, NV:2 * NV] = low

    def product(j, low, high):
        lhs = jnp.concatenate([vector[order[j, s]] for s in range(low, high)], axis=1)
        full = jnp.dot(lhs, weights[j, low * LANES:high * LANES, :], preferred_element_type=jnp.float32)
        return (full[:NV, :LANES] + full[:NV, LANES:]) + (full[NV:, :LANES] + full[NV:, LANES:])

    def own_slots(j):
        return max(0, HB - j), KB - max(0, HB - (rows - 1 - j))

    @pl.loop(0, steps)
    def _(k):
        parity = k % 2
        keep, gain = factors[0, k], factors[1, k]

        @pl.when(has_left)
        def _():
            to_left(parity).start()

        @pl.when(has_right)
        def _():
            to_right(parity).start()

        for b in range(rows):
            now = update[parity, b]
            iterate[b] = iterate[b] + now
            store_vector(HB + b, now)

        def finish(j, applied):
            left_over = resid[j] - applied
            resid[j] = left_over
            update[1 - parity, j] = keep * update[parity, j] + gain * left_over

        for j in range(rows):
            low, high = own_slots(j)
            applied = product(j, low, high)
            if high - low == KB:
                finish(j, applied)
            else:
                partial[j] = applied

        @pl.when(has_left)
        def _():
            to_right(parity).wait_recv()

        @pl.when(has_right)
        def _():
            to_left(parity).wait_recv()

        for b in range(HB):
            store_vector(b, halo[parity, 0, b])
            store_vector(HB + rows + b, halo[parity, 1, b])
        for j in range(rows):
            low, high = own_slots(j)
            if low > 0:
                finish(j, partial[j] + product(j, 0, low))
            elif high < KB:
                finish(j, partial[j] + product(j, high, KB))

        @pl.when(has_left)
        def _():
            to_left(parity).wait_send()

        @pl.when(has_right)
        def _():
            to_right(parity).wait_send()

    for b in range(rows):
        gathered[place * rows + b] = iterate[b] + update[steps % 2, b]

    def piece(where, dest, which):
        return pltpu.make_async_remote_copy(
            src_ref=gathered.at[pl.ds(where * rows, rows)], dst_ref=gathered.at[pl.ds(where * rows, rows)],
            send_sem=c_send.at[which], recv_sem=c_recv.at[where],
            device_id={"group": group, "fold": dest}, device_id_type=MESH,
        )

    for other in (2, 1, 3):
        piece(place, (fold + 2 * other) % FOLDS, other).start()
    piece(place, partner, 0).start()
    for other in (1, 3, 2):
        where = position_of((fold + 2 * other) % FOLDS)
        piece(where, partner, 0).wait_recv()
        piece(where, partner, 3 + other).start()
    for other in range(CHIPS):
        where = position_of((partner + 2 * other) % FOLDS)
        piece(where, partner, 0).wait_recv()

    begin, live = start_of(fold), count_of(fold)
    shift = begin & (LANES - 1)
    base = begin // LANES
    back = (LANES - shift) & (LANES - 1)

    def shifted(m):
        return pltpu.roll(gathered[jnp.minimum(base + m, total_rows - 1)], back, 1)

    here = shifted(0)
    for m in range(slots):
        after = shifted(m + 1)
        value = jnp.where(lane < LANES - shift, here, after)
        out[:, m * LANES:(m + 1) * LANES] = jnp.where(lane + m * LANES < live, value, 0.0)
        here = after

    for which in range(7):
        piece(place, partner, which).wait_send()


def on_device(right_side, initial, counts, columns, blocks):
    folds, groups = lax.axis_size("fold"), lax.axis_size("group")
    slots = right_side.shape[1] // LANES
    owned = blocks.shape[0]
    rows = owned // folds
    factors = step_factors()
    steps = factors.shape[1]
    smem = pl.BlockSpec(memory_space=pltpu.SMEM)
    vmem = pl.BlockSpec(memory_space=pltpu.VMEM)
    f32 = jnp.float32
    dma = pltpu.SemaphoreType.DMA
    return pl.pallas_call(
        functools.partial(kernel, steps, rows, groups),
        out_shape=jax.ShapeDtypeStruct(right_side.shape, f32),
        in_specs=[smem, smem, smem, vmem, vmem, pl.BlockSpec(memory_space=pl.ANY)],
        out_specs=vmem,
        scratch_shapes=[
            pltpu.VMEM(right_side.shape, f32),
            pltpu.VMEM((2, slots + 3, NV, LANES), f32),
            pltpu.VMEM((owned, NV, LANES), f32),
            pltpu.VMEM((folds, rows, NV, LANES), f32),
            pltpu.VMEM((rows, KB, LANES, LANES), f32),
            pltpu.VMEM((rows, KB * LANES, 2 * LANES), jnp.bfloat16),
            pltpu.SMEM((rows, KB), jnp.int32),
            pltpu.VMEM((rows + 2 * HB, 2 * NV, LANES), jnp.bfloat16),
            pltpu.VMEM((2, rows, NV, LANES), f32),
            pltpu.VMEM((rows, NV, LANES), f32),
            pltpu.VMEM((rows, NV, LANES), f32),
            pltpu.VMEM((rows, NV, LANES), f32),
            pltpu.VMEM((2, 2, HB, NV, LANES), f32),
            pltpu.VMEM((owned, NV, LANES), f32),
            dma, dma, dma, dma((8,)), dma((8,)), dma((2, 2)), dma((2, 2)), dma((7,)), dma((8,)),
        ],
        compiler_params=pltpu.CompilerParams(collective_id=0, has_side_effects=True),
    )(jnp.asarray(factors), counts, columns, right_side, initial, blocks)


def solution(mesh):
    placed = (
        P(None, ("group", "fold")),
        P(None, ("group", "fold")),
        P("group", None),
        P("group", None),
        P("group", None, None, None),
    )
    return jax.shard_map(
        on_device, mesh=mesh, in_specs=placed, out_specs=P(None, ("group", "fold")), check_vma=False
    )
```

time: 567 us -> 68.7 us (0.12)
  the two profiles are of different devices: /device:TPU:8 before, /device:TPU:25 now
where the time goes in v1:
time: 68.7 us; the launch traced here: 68.5 us
  Pallas kernels  65.6 us (95%)
  local copies, waits for them, and re-layouts  2.96 us (4%)
    pallas_call x1, Pallas kernels, on_device(): pl.pallas_call(functools.partial(kernel, steps, rows, groups), out_shape=...  65.6 us
    unnamed x2, local copies, waits for them, and re-layouts  2.96 us

profile of v1, /device:TPU:25, one launch (start us, length us, event | category | flops | bytes accessed | tf_op | source)
XLA Modules:
  0.0 68.5 jit_solution(2881701630394315170)
XLA Ops:
  0.0 1.4 %copy.7.columns = s32[64,5]{1,0:T(8,128)} copy(s32[64,5]{0,1:T(8,128)} %param.9) | data formatting | bytes 2560 | tf_op args[3]
  1.4 65.6 %shard_map.64 = f32[16,2048]{1,0:T(8,128)} custom-call(f32[2,12]{1,0:T(2,128)} %constant.2.clone.factors, s32[1,8]{1,0:T(1,128)} %counts.1, s32[64,5]{1,0:T(8,128)} %copy.7.columns, f32[16,2048]{1,0:T(8,128)} %right_side.1, f32[16,2048]{1,0:T(8,128)} %initial.1, f32[64,5,128,128]{3,2,1,0:T(8,128)} %blocks.1), custom_call_target="tpu_custom_call" | custom-call | tf_op jit(solution)/shard_map/pallas_call | solution.py:370
  67.0 1.6 %copy.9 = f32[16,2048]{1,0:T(8,128)} copy(f32[16,2048]{1,0:T(8,128)} %shard_map.64) | data formatting | bytes 262144

commit v2 on v1

v2 whole, which is shorter than its diff:
```python
import functools

import jax
import jax.numpy as jnp
import numpy as np
from jax import lax
from jax.experimental import pallas as pl
from jax.experimental.pallas import tpu as pltpu
from jax.sharding import PartitionSpec as P

MESH = pl.DeviceIdType.MESH
HB = 3
SWEEPS = 3
DEGREE = 4
KB = 5
NV = 16
LANES = 128
FOLDS = 8
CHIPS = 4
DEPTH = 2

upper_bound = 4.5
lower_bound = 1.35


def step_factors():
    theta = (upper_bound + lower_bound) / 2.0
    delta = (upper_bound - lower_bound) / 2.0
    keep, gain = [0.0], [1.0 / theta]
    for sweep in range(SWEEPS):
        ratio = delta / theta
        for step in range(DEGREE - 1):
            ratio_next = 1.0 / (2.0 * theta / delta - ratio)
            keep.append(ratio_next * ratio)
            gain.append(2.0 * ratio_next / delta)
            ratio = ratio_next
        if sweep + 1 < SWEEPS:
            keep.append(0.0)
            gain.append(1.0 / theta)
    return np.array([keep, gain], np.float32)


def split(value):
    high = value.astype(jnp.bfloat16)
    low = (value - high.astype(jnp.float32)).astype(jnp.bfloat16)
    return high, low


def position_of(fold):
    chip, core = fold // 2, fold % 2
    return chip + core * (7 - 2 * chip)


def fold_of(position):
    core = position // 4
    chip = position + core * (7 - 2 * position)
    return 2 * chip + core


def kernel(
    steps, rows, groups, depth,
    factors, counts, columns, right_side, initial, blocks, out,
    raw, aligned, sent, parts, raw_own, raw_left, raw_right, weights, order, all_columns, edge_columns,
    vector, update, resid, mid_update, mid_resid, iterate, partial, halo_update, halo_resid, gathered,
    block_sem, column_sem, edge_send, edge_recv, a_send, a_recv, b_send, b_recv, h_send, h_recv, c_send, c_recv,
):
    group, fold = lax.axis_index("group"), lax.axis_index("fold")
    chip, core = fold // 2, fold % 2
    place = position_of(fold)
    partner = chip * 2 + (1 - core)
    slots = right_side.shape[1] // LANES
    owned = rows * FOLDS
    reach = HB * depth
    outer = HB * (depth - 1)
    wide = rows + 2 * outer
    zero = jnp.zeros((NV, LANES), jnp.float32)

    rank = group * FOLDS + place
    last = groups * FOLDS - 1
    has_left, has_right = rank > 0, rank < last
    left_edge, right_edge = jnp.logical_and(place == 0, has_left), jnp.logical_and(place == FOLDS - 1, has_right)
    left = {"group": group - (7 - place) // 7, "fold": fold_of((place + 7) % 8)}
    right = {"group": group + place // 7, "fold": fold_of((place + 1) % 8)}

    own_blocks = pltpu.make_async_copy(
        blocks.at[pl.ds(place * rows, rows)], raw_own, block_sem.at[0]
    )
    left_blocks = pltpu.make_async_copy(
        blocks.at[pl.ds(jnp.maximum(place * rows - outer, 0), outer)], raw_left, block_sem.at[1]
    )
    right_blocks = pltpu.make_async_copy(
        blocks.at[pl.ds(jnp.minimum(place * rows + rows, owned - outer), outer)],
        raw_right, block_sem.at[2]
    )
    own_columns = pltpu.make_async_copy(columns, all_columns.at[pl.ds(8, owned)], column_sem.at[0])
    own_columns.start()
    own_blocks.start()

    @pl.when(place > 0)
    def _():
        left_blocks.start()

    @pl.when(place < FOLDS - 1)
    def _():
        right_blocks.start()

    barrier = pltpu.get_barrier_semaphore()
    for other in range(1, FOLDS):
        pl.semaphore_signal(barrier, inc=1, device_id={"group": group, "fold": (fold + other) % FOLDS}, device_id_type=MESH)

    @pl.when(left_edge)
    def _():
        pl.semaphore_signal(barrier, inc=1, device_id=left, device_id_type=MESH)

    @pl.when(right_edge)
    def _():
        pl.semaphore_signal(barrier, inc=1, device_id=right, device_id_type=MESH)

    outside = (7 - place) // 7 * ((rank + last) // (last + 1)) + place // 7 * (1 - (rank + 1) // (last + 1))
    pl.semaphore_wait(barrier, FOLDS - 1 + outside)

    def swap(source):
        return pltpu.make_async_remote_copy(
            src_ref=source, dst_ref=raw, send_sem=a_send, recv_sem=a_recv,
            device_id={"group": group, "fold": partner}, device_id_type=MESH,
        )

    @pl.when(core == 0)
    def _():
        swap(initial).start()

    @pl.when(core == 1)
    def _():
        swap(right_side).start()

    def edge_left():
        return [
            pltpu.make_async_remote_copy(
                src_ref=columns.at[pl.ds(0, 8)], dst_ref=edge_columns.at[1],
                send_sem=edge_send.at[0, 0], recv_sem=edge_recv.at[0, 1], device_id=left, device_id_type=MESH,
            ),
            pltpu.make_async_remote_copy(
                src_ref=blocks.at[pl.ds(0, outer)], dst_ref=raw_right,
                send_sem=edge_send.at[1, 0], recv_sem=edge_recv.at[1, 1], device_id=left, device_id_type=MESH,
            ),
        ]

    def edge_right():
        return [
            pltpu.make_async_remote_copy(
                src_ref=columns.at[pl.ds(owned - 8, 8)], dst_ref=edge_columns.at[0],
                send_sem=edge_send.at[0, 1], recv_sem=edge_recv.at[0, 0], device_id=right, device_id_type=MESH,
            ),
            pltpu.make_async_remote_copy(
                src_ref=blocks.at[pl.ds(owned - outer, outer)], dst_ref=raw_left,
                send_sem=edge_send.at[1, 1], recv_sem=edge_recv.at[1, 0], device_id=right, device_id_type=MESH,
            ),
        ]

    @pl.when(left_edge)
    def _():
        for copy in edge_left():
            copy.start()

    @pl.when(right_edge)
    def _():
        for copy in edge_right():
            copy.start()

    lane = lax.broadcasted_iota(jnp.int32, (NV, LANES), 1)

    def start_of(which):
        total = jnp.int32(0)
        for i in range(FOLDS):
            total = total + jnp.where(i < which, counts[0, i], 0)
        return total

    def count_of(which):
        total = jnp.int32(0)
        for i in range(FOLDS):
            total = total + jnp.where(i == which, counts[0, i], 0)
        return total

    def align(source, which):
        start, count = start_of(chip * 2 + which), count_of(chip * 2 + which)
        shift = start & (LANES - 1)
        aligned[which, 0] = zero
        aligned[which, slots + 2] = zero
        before = zero
        for m in range(slots + 1):
            if m < slots:
                now = pltpu.roll(source[:, m * LANES:(m + 1) * LANES], shift, 1)
            else:
                now = zero
            slot = lane + (m * LANES - shift)
            value = jnp.where(lane < shift, before, now)
            live = jnp.logical_and(slot >= 0, slot < count)
            aligned[which, m + 1] = jnp.where(live, value, 0.0)
            before = now

    @pl.when(core == 0)
    def _():
        align(right_side, 0)

    @pl.when(core == 1)
    def _():
        align(initial, 1)

    swap(initial).wait()

    @pl.when(core == 0)
    def _():
        align(raw, 1)

    @pl.when(core == 1)
    def _():
        align(raw, 0)

    first = [start_of(chip * 2) // LANES, start_of(chip * 2 + 1) // LANES]

    def row_block(index):
        at = [jnp.clip(index - first[i], -1, slots + 1) + 1 for i in range(2)]
        return aligned[0, at[0]] + aligned[1, at[1]]

    def message(other):
        dest = (fold + other) % FOLDS
        where = position_of(dest) * rows
        return where, pltpu.make_async_remote_copy(
            src_ref=sent.at[pl.ds(where, rows)], dst_ref=parts.at[fold],
            send_sem=b_send.at[other], recv_sem=b_recv.at[fold],
            device_id={"group": group, "fold": dest}, device_id_type=MESH,
        )

    def arrival(source):
        return pltpu.make_async_remote_copy(
            src_ref=sent.at[pl.ds(0, rows)], dst_ref=parts.at[source],
            send_sem=b_send.at[0], recv_sem=b_recv.at[source],
            device_id={"group": group, "fold": fold}, device_id_type=MESH,
        )

    for other in (4, 3, 5, 2, 6, 1, 7):
        where, copy = message(other)
        for b in range(rows):
            sent[where + b] = row_block(where + b)
        copy.start()
    for b in range(rows):
        parts[fold, b] = row_block(place * rows + b)

    def prepare(source, low, high):
        @pl.loop(low, high)
        def _(e):
            at_row = place * rows + e - outer + 8
            move = jnp.where(at_row < 8, -owned, jnp.where(at_row >= owned + 8, owned, 0)) - place * rows + outer
            column = [all_columns[at_row, k] for k in range(KB)]
            ranks = []
            for k in range(KB):
                r = jnp.int32(0)
                for other in range(KB):
                    if other != k:
                        ahead = column[other] <= column[k] if other < k else column[other] < column[k]
                        r = r + ahead.astype(jnp.int32)
                ranks.append(r)
            for s in range(KB):
                from_slot, at = jnp.int32(0), jnp.int32(0)
                for k in range(KB):
                    from_slot = from_slot + jnp.where(ranks[k] == s, k, 0)
                    at = at + jnp.where(ranks[k] == s, column[k], 0)
                order[e, s] = jnp.clip(at + move, 0, rows + 2 * reach - 1)
                high_part, low_part = split(source[e - low, from_slot].T)
                weights[e, s * LANES:(s + 1) * LANES, 0:LANES] = high_part
                weights[e, s * LANES:(s + 1) * LANES, LANES:2 * LANES] = low_part

    def absent(low, side):
        for e in range(low, low + outer):
            for s in range(KB):
                order[e, s] = 0
            weights[e] = jnp.zeros((KB * LANES, 2 * LANES), jnp.bfloat16)
        for parity in range(2):
            for b in range(reach):
                halo_update[parity, side, b] = zero
            for b in range(outer):
                halo_resid[parity, side, b] = zero

    own_columns.wait()
    own_blocks.wait()
    prepare(raw_own, outer, outer + rows)

    @pl.when(place > 0)
    def _():
        left_blocks.wait()
        prepare(raw_left, 0, outer)

    @pl.when(place < FOLDS - 1)
    def _():
        right_blocks.wait()
        prepare(raw_right, outer + rows, wide)

    @pl.when(jnp.logical_not(has_left))
    def _():
        absent(0, 0)

    @pl.when(jnp.logical_not(has_right))
    def _():
        absent(outer + rows, 1)

    def store_vector(which, index, value):
        high, low = split(value)
        vector[which, index, 0:NV] = high
        vector[which, index, NV:2 * NV] = low

    for other in range(1, FOLDS):
        arrival((fold + other) % FOLDS).wait_recv()
    for b in range(rows):
        resid[0, b] = (parts[0, b] + parts[2, b]) + (parts[4, b] + parts[6, b])
        begun = (parts[1, b] + parts[3, b]) + (parts[5, b] + parts[7, b])
        update[0, b] = begun
        iterate[b] = zero
        store_vector(0, reach + b, begun)

    def exchange(parity):
        def copy(source, target, side, which):
            return pltpu.make_async_remote_copy(
                src_ref=source, dst_ref=target,
                send_sem=h_send.at[parity, side, which], recv_sem=h_recv.at[parity, 1 - side, which],
                device_id=right if side else left, device_id_type=MESH,
            )

        return [
            [
                copy(update.at[parity, pl.ds(0, reach)], halo_update.at[parity, 1], 0, 0),
                copy(resid.at[parity, pl.ds(0, outer)], halo_resid.at[parity, 1], 0, 1),
            ],
            [
                copy(update.at[parity, pl.ds(rows - reach, reach)], halo_update.at[parity, 0], 1, 0),
                copy(resid.at[parity, pl.ds(rows - outer, outer)], halo_resid.at[parity, 0], 1, 1),
            ],
        ]

    def send(parity):
        copies = exchange(parity)
        for which in range(2):
            @pl.when(has_left)
            def _():
                copies[0][which].start()

            @pl.when(has_right)
            def _():
                copies[1][which].start()

    def receive(parity, which):
        copies = exchange(parity)

        @pl.when(has_left)
        def _():
            copies[1][which].wait_recv()

        @pl.when(has_right)
        def _():
            copies[0][which].wait_recv()

    send(0)

    for other in range(1, FOLDS):
        message(other)[1].wait_send()

    def edge_done(side):
        arrived = (edge_left if side else edge_right)()
        arrived[0].wait_recv()
        into = pltpu.make_async_copy(
            edge_columns.at[side], all_columns.at[pl.ds(side * (owned + 8), 8)], column_sem.at[1 + side]
        )
        into.start()
        into.wait()
        arrived[1].wait_recv()
        prepare(raw_right if side else raw_left, side * (outer + rows), side * (outer + rows) + outer)

    @pl.when(left_edge)
    def _():
        edge_done(0)
        for copy in edge_left():
            copy.wait_send()

    @pl.when(right_edge)
    def _():
        edge_done(1)
        for copy in edge_right():
            copy.wait_send()

    def product(which, e, low, high):
        lhs = jnp.concatenate([vector[which, order[e, s]] for s in range(low, high)], axis=1)
        full = jnp.dot(lhs, weights[e, low * LANES:high * LANES, :], preferred_element_type=jnp.float32)
        return (full[:NV, :LANES] + full[:NV, LANES:]) + (full[NV:, :LANES] + full[NV:, LANES:])

    def own_slots(j):
        return max(0, HB - j), KB - max(0, HB - (rows - 1 - j))

    rounds = steps // depth

    @pl.loop(0, rounds)
    def _(turn):
        parity = turn % 2

        for level in range(depth):
            now, later = level % 2, (level + 1) % 2
            k = turn * depth + level
            keep, gain = factors[0, k], factors[1, k]

            def finish(e, applied):
                own = e - outer
                inside = 0 <= own < rows
                if level > 0:
                    old, left_over = mid_update[e], mid_resid[e]
                elif inside:
                    old, left_over = update[parity, own], resid[parity, own]
                elif own < 0:
                    old, left_over = halo_update[parity, 0, e + HB], halo_resid[parity, 0, e]
                else:
                    old, left_over = halo_update[parity, 1, own - rows], halo_resid[parity, 1, own - rows]
                left_over = left_over - applied
                fresh = keep * old + gain * left_over
                if inside:
                    iterate[own] = iterate[own] + old
                if level == depth - 1:
                    update[1 - parity, own] = fresh
                    resid[1 - parity, own] = left_over
                else:
                    mid_update[e] = fresh
                    mid_resid[e] = left_over
                store_vector(later, e + HB, fresh)

            margin = HB * (depth - 1 - level)
            if level > 0:
                for e in range(outer - margin, outer + rows + margin):
                    finish(e, product(now, e, 0, KB))
                continue

            for j in range(rows):
                low, high = own_slots(j)
                applied = product(now, j + outer, low, high)
                if high - low == KB:
                    finish(j + outer, applied)
                else:
                    partial[j] = applied
            receive(parity, 0)
            for b in range(reach):
                store_vector(now, b, halo_update[parity, 0, b])
                store_vector(now, reach + rows + b, halo_update[parity, 1, b])
            for j in range(rows):
                low, high = own_slots(j)
                if low > 0:
                    finish(j + outer, partial[j] + product(now, j + outer, 0, low))
                elif high < KB:
                    finish(j + outer, partial[j] + product(now, j + outer, high, KB))
            receive(parity, 1)
            for e in list(range(outer)) + list(range(outer + rows, wide)):
                finish(e, product(now, e, 0, KB))

        copies = exchange(parity)
        for which in range(2):
            @pl.when(has_left)
            def _():
                copies[0][which].wait_send()

            @pl.when(has_right)
            def _():
                copies[1][which].wait_send()

        @pl.when(turn + 1 < rounds)
        def _():
            send(1 - parity)

    for b in range(rows):
        gathered[place * rows + b] = iterate[b] + update[rounds % 2, b]

    def piece(where, dest, which):
        return pltpu.make_async_remote_copy(
            src_ref=gathered.at[pl.ds(where * rows, rows)], dst_ref=gathered.at[pl.ds(where * rows, rows)],
            send_sem=c_send.at[which], recv_sem=c_recv.at[where],
            device_id={"group": group, "fold": dest}, device_id_type=MESH,
        )

    for other in (2, 1, 3):
        piece(place, (fold + 2 * other) % FOLDS, other).start()
    piece(place, partner, 0).start()
    for other in (1, 3, 2):
        where = position_of((fold + 2 * other) % FOLDS)
        piece(where, partner, 0).wait_recv()
        piece(where, partner, 3 + other).start()
    for other in range(CHIPS):
        where = position_of((partner + 2 * other) % FOLDS)
        piece(where, partner, 0).wait_recv()

    begin, live = start_of(fold), count_of(fold)
    shift = begin & (LANES - 1)
    base = begin // LANES
    back = (LANES - shift) & (LANES - 1)

    def shifted(m):
        return pltpu.roll(gathered[jnp.minimum(base + m, owned - 1)], back, 1)

    here = shifted(0)
    for m in range(slots):
        after = shifted(m + 1)
        value = jnp.where(lane < LANES - shift, here, after)
        out[:, m * LANES:(m + 1) * LANES] = jnp.where(lane + m * LANES < live, value, 0.0)
        here = after

    for which in range(7):
        piece(place, partner, which).wait_send()


def on_device(right_side, initial, counts, columns, blocks):
    folds, groups = lax.axis_size("fold"), lax.axis_size("group")
    slots = right_side.shape[1] // LANES
    owned = blocks.shape[0]
    rows = owned // folds
    factors = step_factors()
    steps, depth = factors.shape[1], DEPTH
    reach, outer = HB * depth, HB * (depth - 1)
    smem = pl.BlockSpec(memory_space=pltpu.SMEM)
    vmem = pl.BlockSpec(memory_space=pltpu.VMEM)
    anywhere = pl.BlockSpec(memory_space=pl.ANY)
    f32, i32 = jnp.float32, jnp.int32
    dma = pltpu.SemaphoreType.DMA

    def vectors(*shape):
        return pltpu.VMEM(shape + (NV, LANES), f32)

    return pl.pallas_call(
        functools.partial(kernel, steps, rows, groups, depth),
        out_shape=jax.ShapeDtypeStruct(right_side.shape, f32),
        in_specs=[smem, smem, anywhere, vmem, vmem, anywhere],
        out_specs=vmem,
        scratch_shapes=[
            pltpu.VMEM(right_side.shape, f32),
            vectors(2, slots + 3),
            vectors(owned),
            vectors(folds, rows),
            pltpu.VMEM((rows, KB, LANES, LANES), f32),
            pltpu.VMEM((outer, KB, LANES, LANES), f32),
            pltpu.VMEM((outer, KB, LANES, LANES), f32),
            pltpu.VMEM((rows + 2 * outer, KB * LANES, 2 * LANES), jnp.bfloat16),
            pltpu.SMEM((rows + 2 * outer, KB), i32),
            pltpu.SMEM((owned + 16, KB), i32),
            pltpu.VMEM((2, 8, KB), i32),
            pltpu.VMEM((2, rows + 2 * reach, 2 * NV, LANES), jnp.bfloat16),
            vectors(2, rows),
            vectors(2, rows),
            vectors(rows + 2 * outer),
            vectors(rows + 2 * outer),
            vectors(rows),
            vectors(rows),
            vectors(2, 2, reach),
            vectors(2, 2, outer),
            vectors(owned),
            dma((3,)), dma((3,)), dma((2, 2)), dma((2, 2)), dma, dma, dma((8,)), dma((8,)),
            dma((2, 2, 2)), dma((2, 2, 2)), dma((7,)), dma((8,)),
        ],
        compiler_params=pltpu.CompilerParams(collective_id=0, has_side_effects=True),
    )(jnp.asarray(factors), counts, columns, right_side, initial, blocks)


def solution(mesh):
    placed = (
        P(None, ("group", "fold")),
        P(None, ("group", "fold")),
        P("group", None),
        P("group", None),
        P("group", None, None, None),
    )
    return jax.shard_map(
        on_device, mesh=mesh, in_specs=placed, out_specs=P(None, ("group", "fold")), check_vma=False
    )
```

time: 68.7 us -> 69.9 us (1.017)
  Pallas kernels: 65.6 us -> 66.8 us
    pallas_call x1, Pallas kernels: 65.6 us -> 66.8 us  [on_device(): pl.pallas_call(functools.partial(kernel, steps, rows, groups, depth), out...]
where the time goes in v2:
time: 69.9 us; the launch traced here: 69.7 us
  Pallas kernels  66.8 us (96%)
  local copies, waits for them, and re-layouts  2.96 us (4%)
    pallas_call x1, Pallas kernels, on_device(): pl.pallas_call(functools.partial(kernel, steps, rows, groups, depth), out...  66.8 us
    unnamed x2, local copies, waits for them, and re-layouts  2.96 us

profile of v2, /device:TPU:25, one launch (start us, length us, event | category | flops | bytes accessed | tf_op | source)
XLA Modules:
  0.0 69.7 jit_solution(5388796737228896667)
XLA Ops:
  0.0 1.4 %copy.7.columns = s32[64,5]{1,0:T(8,128)} copy(s32[64,5]{0,1:T(8,128)} %param.9) | data formatting | bytes 2560 | tf_op args[3]
  1.4 66.8 %shard_map.64 = f32[16,2048]{1,0:T(8,128)} custom-call(f32[2,12]{1,0:T(2,128)} %constant.2.clone.factors, s32[1,8]{1,0:T(1,128)} %counts.1, s32[64,5]{1,0:T(8,128)} %copy.7.columns, f32[16,2048]{1,0:T(8,128)} %right_side.1, f32[16,2048]{1,0:T(8,128)} %initial.1, f32[64,5,128,128]{3,2,1,0:T(8,128)} %blocks.1), custom_call_target="tpu_custom_call" | custom-call | tf_op jit(solution)/shard_map/pallas_call | solution.py:529
  68.2 1.6 %copy.9 = f32[16,2048]{1,0:T(8,128)} copy(f32[16,2048]{1,0:T(8,128)} %shard_map.64) | data formatting | bytes 262144

commit v3 on v2

--- a/solution.py
+++ b/solution.py
@@ -2,7 +2,6 @@
 
 import jax
 import jax.numpy as jnp
-import numpy as np
 from jax import lax
 from jax.experimental import pallas as pl
 from jax.experimental.pallas import tpu as pltpu
@@ -27,17 +26,13 @@
     theta = (upper_bound + lower_bound) / 2.0
     delta = (upper_bound - lower_bound) / 2.0
     keep, gain = [0.0], [1.0 / theta]
-    for sweep in range(SWEEPS):
-        ratio = delta / theta
-        for step in range(DEGREE - 1):
-            ratio_next = 1.0 / (2.0 * theta / delta - ratio)
-            keep.append(ratio_next * ratio)
-            gain.append(2.0 * ratio_next / delta)
-            ratio = ratio_next
-        if sweep + 1 < SWEEPS:
-            keep.append(0.0)
-            gain.append(1.0 / theta)
-    return np.array([keep, gain], np.float32)
+    ratio = delta / theta
+    for step in range(DEGREE - 1):
+        ratio_next = 1.0 / (2.0 * theta / delta - ratio)
+        keep.append(ratio_next * ratio)
+        gain.append(2.0 * ratio_next / delta)
+        ratio = ratio_next
+    return keep, gain
 
 
 def split(value):
@@ -58,10 +53,10 @@
 
 
 def kernel(
-    steps, rows, groups, depth,
-    factors, counts, columns, right_side, initial, blocks, out,
-    raw, aligned, sent, parts, raw_own, raw_left, raw_right, weights, order, all_columns, edge_columns,
-    vector, update, resid, mid_update, mid_resid, iterate, partial, halo_update, halo_resid, gathered,
+    rows, groups, depth,
+    counts_in, columns, right_side, initial, blocks, out,
+    counts, mine, raw, aligned, sent, parts, raw_own, raw_left, raw_right, weights, order, all_columns, edge_columns,
+    vector_even, vector_odd, update, resid, mid_update, mid_resid, iterate, partial, halo_update, halo_resid, gathered,
     block_sem, column_sem, edge_send, edge_recv, a_send, a_recv, b_send, b_recv, h_send, h_recv, c_send, c_recv,
 ):
     group, fold = lax.axis_index("group"), lax.axis_index("fold")
@@ -92,7 +87,33 @@
         blocks.at[pl.ds(jnp.minimum(place * rows + rows, owned - outer), outer)],
         raw_right, block_sem.at[2]
     )
-    own_columns = pltpu.make_async_copy(columns, all_columns.at[pl.ds(8, owned)], column_sem.at[0])
+    own_columns = pltpu.make_async_copy(columns, all_columns.at[1], column_sem.at[0])
+    barrier = pltpu.get_barrier_semaphore()
+    @pl.when(left_edge)
+    def _():
+        pl.semaphore_signal(barrier, inc=1, device_id=left, device_id_type=MESH)
+
+    @pl.when(right_edge)
+    def _():
+        pl.semaphore_signal(barrier, inc=1, device_id=right, device_id_type=MESH)
+
+    for other in (4, 3, 5, 2, 6, 1, 7):
+        pl.semaphore_signal(barrier, inc=1, device_id={"group": group, "fold": (fold + other) % FOLDS}, device_id_type=MESH)
+
+    own_counts = pltpu.make_async_copy(counts_in, counts, column_sem.at[3])
+    own_counts.start()
+
+    def own_slots_copy(source):
+        return pltpu.make_async_copy(source, mine, block_sem.at[3])
+
+    @pl.when(core == 0)
+    def _():
+        own_slots_copy(right_side).start()
+
+    @pl.when(core == 1)
+    def _():
+        own_slots_copy(initial).start()
+
     own_columns.start()
     own_blocks.start()
 
@@ -103,18 +124,6 @@
     @pl.when(place < FOLDS - 1)
     def _():
         right_blocks.start()
-
-    barrier = pltpu.get_barrier_semaphore()
-    for other in range(1, FOLDS):
-        pl.semaphore_signal(barrier, inc=1, device_id={"group": group, "fold": (fold + other) % FOLDS}, device_id_type=MESH)
-
-    @pl.when(left_edge)
-    def _():
-        pl.semaphore_signal(barrier, inc=1, device_id=left, device_id_type=MESH)
-
-    @pl.when(right_edge)
-    def _():
-        pl.semaphore_signal(barrier, inc=1, device_id=right, device_id_type=MESH)
 
     outside = (7 - place) // 7 * ((rank + last) // (last + 1)) + place // 7 * (1 - (rank + 1) // (last + 1))
     pl.semaphore_wait(barrier, FOLDS - 1 + outside)
@@ -136,7 +145,7 @@
     def edge_left():
         return [
             pltpu.make_async_remote_copy(
-                src_ref=columns.at[pl.ds(0, 8)], dst_ref=edge_columns.at[1],
+                src_ref=columns, dst_ref=edge_columns.at[1],
                 send_sem=edge_send.at[0, 0], recv_sem=edge_recv.at[0, 1], device_id=left, device_id_type=MESH,
             ),
             pltpu.make_async_remote_copy(
@@ -148,7 +157,7 @@
     def edge_right():
         return [
             pltpu.make_async_remote_copy(
-                src_ref=columns.at[pl.ds(owned - 8, 8)], dst_ref=edge_columns.at[0],
+                src_ref=columns, dst_ref=edge_columns.at[0],
                 send_sem=edge_send.at[0, 1], recv_sem=edge_recv.at[0, 0], device_id=right, device_id_type=MESH,
             ),
             pltpu.make_async_remote_copy(
@@ -198,13 +207,16 @@
             aligned[which, m + 1] = jnp.where(live, value, 0.0)
             before = now
 
+    own_counts.wait()
+    own_slots_copy(initial).wait()
+
     @pl.when(core == 0)
     def _():
-        align(right_side, 0)
+        align(mine, 0)
 
     @pl.when(core == 1)
     def _():
-        align(initial, 1)
+        align(mine, 1)
 
     swap(initial).wait()
 
@@ -231,6 +243,10 @@
             device_id={"group": group, "fold": dest}, device_id_type=MESH,
         )
 
+    def reachable(source, dest):
+        low = jnp.logical_and(source == CHIPS - 1, dest < FOLDS // 2)
+        return jnp.logical_not(jnp.logical_or(low, jnp.logical_and(source == 0, dest >= FOLDS // 2)))
+
     def arrival(source):
         return pltpu.make_async_remote_copy(
             src_ref=sent.at[pl.ds(0, rows)], dst_ref=parts.at[source],
@@ -242,16 +258,29 @@
         where, copy = message(other)
         for b in range(rows):
             sent[where + b] = row_block(where + b)
-        copy.start()
+
+        @pl.when(reachable(chip, position_of((fold + other) % FOLDS)))
+        def _():
+            copy.start()
+
     for b in range(rows):
         parts[fold, b] = row_block(place * rows + b)
+    for other in range(1, FOLDS):
+        source = (fold + other) % FOLDS
+
+        @pl.when(jnp.logical_not(reachable(source // 2, place)))
+        def _():
+            for b in range(rows):
+                parts[source, b] = zero
+
 
     def prepare(source, low, high):
         @pl.loop(low, high)
         def _(e):
-            at_row = place * rows + e - outer + 8
-            move = jnp.where(at_row < 8, -owned, jnp.where(at_row >= owned + 8, owned, 0)) - place * rows + outer
-            column = [all_columns[at_row, k] for k in range(KB)]
+            at_row = place * rows + e - outer + owned
+            owner, within = at_row // owned, at_row % owned
+            move = (owner - 1) * owned - place * rows + outer
+            column = [all_columns[owner, k, within] for k in range(KB)]
             ranks = []
             for k in range(KB):
                 r = jnp.int32(0)
@@ -303,13 +332,20 @@
     def _():
         absent(outer + rows, 1)
 
+    vectors = [vector_even, vector_odd]
+
     def store_vector(which, index, value):
         high, low = split(value)
-        vector[which, index, 0:NV] = high
-        vector[which, index, NV:2 * NV] = low
+        vectors[which][index, 0:NV] = high
+        vectors[which][index, NV:2 * NV] = low
 
     for other in range(1, FOLDS):
-        arrival((fold + other) % FOLDS).wait_recv()
+        source = (fold + other) % FOLDS
+
+        @pl.when(reachable(source // 2, place))
+        def _():
+            arrival(source).wait_recv()
+
     for b in range(rows):
         resid[0, b] = (parts[0, b] + parts[2, b]) + (parts[4, b] + parts[6, b])
         begun = (parts[1, b] + parts[3, b]) + (parts[5, b] + parts[7, b])
@@ -361,40 +397,34 @@
     send(0)
 
     for other in range(1, FOLDS):
-        message(other)[1].wait_send()
+        @pl.when(reachable(chip, position_of((fold + other) % FOLDS)))
+        def _():
+            message(other)[1].wait_send()
+
 
     def edge_done(side):
         arrived = (edge_left if side else edge_right)()
         arrived[0].wait_recv()
         into = pltpu.make_async_copy(
-            edge_columns.at[side], all_columns.at[pl.ds(side * (owned + 8), 8)], column_sem.at[1 + side]
+            edge_columns.at[side], all_columns.at[2 * side], column_sem.at[1 + side]
         )
         into.start()
         into.wait()
         arrived[1].wait_recv()
         prepare(raw_right if side else raw_left, side * (outer + rows), side * (outer + rows) + outer)
-
-    @pl.when(left_edge)
-    def _():
-        edge_done(0)
-        for copy in edge_left():
+        for copy in (edge_right if side else edge_left)():
             copy.wait_send()
 
-    @pl.when(right_edge)
-    def _():
-        edge_done(1)
-        for copy in edge_right():
-            copy.wait_send()
-
     def product(which, e, low, high):
-        lhs = jnp.concatenate([vector[which, order[e, s]] for s in range(low, high)], axis=1)
+        lhs = jnp.concatenate([vectors[which][order[e, s]] for s in range(low, high)], axis=1)
         full = jnp.dot(lhs, weights[e, low * LANES:high * LANES, :], preferred_element_type=jnp.float32)
         return (full[:NV, :LANES] + full[:NV, LANES:]) + (full[NV:, :LANES] + full[NV:, LANES:])
 
     def own_slots(j):
         return max(0, HB - j), KB - max(0, HB - (rows - 1 - j))
 
-    rounds = steps // depth
+    keeps, gains = step_factors()
+    rounds = SWEEPS * DEGREE // depth
 
     @pl.loop(0, rounds)
     def _(turn):
@@ -402,8 +432,11 @@
 
         for level in range(depth):
             now, later = level % 2, (level + 1) % 2
-            k = turn * depth + level
-            keep, gain = factors[0, k], factors[1, k]
+            keep, gain = jnp.float32(keeps[level]), jnp.float32(gains[level])
+            for phase in range(1, DEGREE // depth):
+                chosen = turn % (DEGREE // depth) == phase
+                keep = jnp.where(chosen, jnp.float32(keeps[phase * depth + level]), keep)
+                gain = jnp.where(chosen, jnp.float32(gains[phase * depth + level]), gain)
 
             def finish(e, applied):
                 own = e - outer
@@ -452,6 +485,15 @@
                 elif high < KB:
                     finish(j + outer, partial[j] + product(now, j + outer, high, KB))
             receive(parity, 1)
+
+            @pl.when(jnp.logical_and(turn == 0, left_edge))
+            def _():
+                edge_done(0)
+
+            @pl.when(jnp.logical_and(turn == 0, right_edge))
+            def _():
+                edge_done(1)
+
             for e in list(range(outer)) + list(range(outer + rows, wide)):
                 finish(e, product(now, e, 0, KB))
 
@@ -514,10 +556,8 @@
     slots = right_side.shape[1] // LANES
     owned = blocks.shape[0]
     rows = owned // folds
-    factors = step_factors()
-    steps, depth = factors.shape[1], DEPTH
+    depth = DEPTH
     reach, outer = HB * depth, HB * (depth - 1)
-    smem = pl.BlockSpec(memory_space=pltpu.SMEM)
     vmem = pl.BlockSpec(memory_space=pltpu.VMEM)
     anywhere = pl.BlockSpec(memory_space=pl.ANY)
     f32, i32 = jnp.float32, jnp.int32
@@ -527,11 +567,13 @@
         return pltpu.VMEM(shape + (NV, LANES), f32)
 
     return pl.pallas_call(
-        functools.partial(kernel, steps, rows, groups, depth),
+        functools.partial(kernel, rows, groups, depth),
         out_shape=jax.ShapeDtypeStruct(right_side.shape, f32),
-        in_specs=[smem, smem, anywhere, vmem, vmem, anywhere],
+        in_specs=[anywhere] * 5,
         out_specs=vmem,
         scratch_shapes=[
+            pltpu.SMEM(counts.shape, i32),
+            pltpu.VMEM(right_side.shape, f32),
             pltpu.VMEM(right_side.shape, f32),
             vectors(2, slots + 3),
             vectors(owned),
@@ -541,9 +583,10 @@
             pltpu.VMEM((outer, KB, LANES, LANES), f32),
             pltpu.VMEM((rows + 2 * outer, KB * LANES, 2 * LANES), jnp.bfloat16),
             pltpu.SMEM((rows + 2 * outer, KB), i32),
-            pltpu.SMEM((owned + 16, KB), i32),
-            pltpu.VMEM((2, 8, KB), i32),
-            pltpu.VMEM((2, rows + 2 * reach, 2 * NV, LANES), jnp.bfloat16),
+            pltpu.SMEM((3, KB, owned), i32),
+            pltpu.VMEM((2, KB, owned), i32),
+            pltpu.VMEM((rows + 2 * reach, 2 * NV, LANES), jnp.bfloat16),
+            pltpu.VMEM((rows + 2 * reach, 2 * NV, LANES), jnp.bfloat16),
             vectors(2, rows),
             vectors(2, rows),
             vectors(rows + 2 * outer),
@@ -553,11 +596,11 @@
             vectors(2, 2, reach),
             vectors(2, 2, outer),
             vectors(owned),
-            dma((3,)), dma((3,)), dma((2, 2)), dma((2, 2)), dma, dma, dma((8,)), dma((8,)),
+            dma((4,)), dma((4,)), dma((2, 2)), dma((2, 2)), dma, dma, dma((8,)), dma((8,)),
             dma((2, 2, 2)), dma((2, 2, 2)), dma((7,)), dma((8,)),
         ],
         compiler_params=pltpu.CompilerParams(collective_id=0, has_side_effects=True),
-    )(jnp.asarray(factors), counts, columns, right_side, initial, blocks)
+    )(counts, columns.T, right_side, initial, blocks)
 
 
 def solution(mesh):

time: 69.9 us -> 55.7 us (0.80)
  Pallas kernels: 66.8 us -> 54 us
  local copies, waits for them, and re-layouts: 2.96 us -> 1.57 us
    pallas_call x1, Pallas kernels: 66.8 us -> 54 us  [on_device(): pl.pallas_call(functools.partial(kernel, rows, groups, depth), out_shape=...]
    unnamed x2 -> x1, local copies, waits for them, and re-layouts: 2.96 us -> 1.57 us
where the time goes in v3:
time: 55.7 us; the launch traced here: 55.6 us
  Pallas kernels  54 us (97%)
  local copies, waits for them, and re-layouts  1.57 us (3%)
    pallas_call x1, Pallas kernels, on_device(): pl.pallas_call(functools.partial(kernel, rows, groups, depth), out_shape=...  54 us
    unnamed x1, local copies, waits for them, and re-layouts  1.57 us

profile of v3, /device:TPU:25, one launch (start us, length us, event | category | flops | bytes accessed | tf_op | source)
XLA Modules:
  0.0 55.6 jit_solution(9531483549103378146)
XLA Ops:
  0.0 54.0 %shard_map.55 = f32[16,2048]{1,0:T(8,128)} custom-call(s32[1,8]{1,0:T(1,128)} %counts_in.1, s32[5,64]{1,0:T(8,128)} %bitcast.1, f32[16,2048]{1,0:T(8,128)} %right_side.1, f32[16,2048]{1,0:T(8,128)} %initial.1, f32[64,5,128,128]{3,2,1,0:T(8,128)} %blocks.1), custom_call_target="tpu_custom_call" | custom-call | tf_op jit(solution)/shard_map/pallas_call | solution.py:569
  54.1 1.6 %copy.7 = f32[16,2048]{1,0:T(8,128)} copy(f32[16,2048]{1,0:T(8,128)} %shard_map.55) | data formatting | bytes 262144

commit v4 on v3

--- a/solution.py
+++ b/solution.py
@@ -17,6 +17,7 @@
 FOLDS = 8
 CHIPS = 4
 DEPTH = 2
+EARLY = 2
 
 upper_bound = 4.5
 lower_bound = 1.35
@@ -55,7 +56,7 @@
 def kernel(
     rows, groups, depth,
     counts_in, columns, right_side, initial, blocks, out,
-    counts, mine, raw, aligned, sent, parts, raw_own, raw_left, raw_right, weights, order, all_columns, edge_columns,
+    counts, mine, raw, aligned, sent, parts, raw_own, raw_left, raw_right, left_last, right_last, weights, order, all_columns, edge_columns,
     vector_even, vector_odd, update, resid, mid_update, mid_resid, iterate, partial, halo_update, halo_resid, gathered,
     block_sem, column_sem, edge_send, edge_recv, a_send, a_recv, b_send, b_recv, h_send, h_recv, c_send, c_recv,
 ):
@@ -80,13 +81,18 @@
     own_blocks = pltpu.make_async_copy(
         blocks.at[pl.ds(place * rows, rows)], raw_own, block_sem.at[0]
     )
-    left_blocks = pltpu.make_async_copy(
-        blocks.at[pl.ds(jnp.maximum(place * rows - outer, 0), outer)], raw_left, block_sem.at[1]
-    )
-    right_blocks = pltpu.make_async_copy(
-        blocks.at[pl.ds(jnp.minimum(place * rows + rows, owned - outer), outer)],
-        raw_right, block_sem.at[2]
-    )
+    most = outer - 1
+    raw_last = [left_last, right_last]
+
+    def beside(side):
+        begin = jnp.minimum(place * rows + rows, owned - outer) if side else jnp.maximum(place * rows - outer, 0)
+        return [
+            pltpu.make_async_copy(
+                blocks.at[pl.ds(begin, most)], (raw_right if side else raw_left), block_sem.at[1 + 2 * side]
+            ),
+            pltpu.make_async_copy(blocks.at[begin + most], raw_last[side], block_sem.at[2 + 2 * side]),
+        ]
+
     own_columns = pltpu.make_async_copy(columns, all_columns.at[1], column_sem.at[0])
     barrier = pltpu.get_barrier_semaphore()
     @pl.when(left_edge)
@@ -104,7 +110,7 @@
     own_counts.start()
 
     def own_slots_copy(source):
-        return pltpu.make_async_copy(source, mine, block_sem.at[3])
+        return pltpu.make_async_copy(source, mine, block_sem.at[5])
 
     @pl.when(core == 0)
     def _():
@@ -119,11 +125,13 @@
 
     @pl.when(place > 0)
     def _():
-        left_blocks.start()
+        for copy in beside(0):
+            copy.start()
 
     @pl.when(place < FOLDS - 1)
     def _():
-        right_blocks.start()
+        for copy in beside(1):
+            copy.start()
 
     outside = (7 - place) // 7 * ((rank + last) // (last + 1)) + place // 7 * (1 - (rank + 1) // (last + 1))
     pl.semaphore_wait(barrier, FOLDS - 1 + outside)
@@ -142,39 +150,35 @@
     def _():
         swap(right_side).start()
 
-    def edge_left():
+    def edge(side):
+        begin = owned - outer if side else 0
+        target = 1 - side
+        refs = [
+            (columns, edge_columns.at[target]),
+            (blocks.at[pl.ds(begin, most)], (raw_right if target else raw_left)),
+            (blocks.at[begin + most, pl.ds(0, EARLY)], raw_last[target].at[pl.ds(0, EARLY)]),
+            (blocks.at[begin + most, pl.ds(EARLY, KB - EARLY)], raw_last[target].at[pl.ds(EARLY, KB - EARLY)]),
+        ]
         return [
             pltpu.make_async_remote_copy(
-                src_ref=columns, dst_ref=edge_columns.at[1],
-                send_sem=edge_send.at[0, 0], recv_sem=edge_recv.at[0, 1], device_id=left, device_id_type=MESH,
-            ),
-            pltpu.make_async_remote_copy(
-                src_ref=blocks.at[pl.ds(0, outer)], dst_ref=raw_right,
-                send_sem=edge_send.at[1, 0], recv_sem=edge_recv.at[1, 1], device_id=left, device_id_type=MESH,
-            ),
+                src_ref=source, dst_ref=dest, send_sem=edge_send.at[i, side], recv_sem=edge_recv.at[i, target],
+                device_id=right if side else left, device_id_type=MESH,
+            )
+            for i, (source, dest) in enumerate(refs)
         ]
 
-    def edge_right():
-        return [
-            pltpu.make_async_remote_copy(
-                src_ref=columns, dst_ref=edge_columns.at[0],
-                send_sem=edge_send.at[0, 1], recv_sem=edge_recv.at[0, 0], device_id=right, device_id_type=MESH,
-            ),
-            pltpu.make_async_remote_copy(
-                src_ref=blocks.at[pl.ds(owned - outer, outer)], dst_ref=raw_left,
-                send_sem=edge_send.at[1, 1], recv_sem=edge_recv.at[1, 0], device_id=right, device_id_type=MESH,
-            ),
-        ]
-
-    @pl.when(left_edge)
-    def _():
-        for copy in edge_left():
-            copy.start()
-
-    @pl.when(right_edge)
-    def _():
-        for copy in edge_right():
-            copy.start()
+    def edge_start(low, high):
+        @pl.when(left_edge)
+        def _():
+            for copy in edge(0)[low:high]:
+                copy.start()
+
+        @pl.when(right_edge)
+        def _():
+            for copy in edge(1)[low:high]:
+                copy.start()
+
+    edge_start(0, 3)
 
     lane = lax.broadcasted_iota(jnp.int32, (NV, LANES), 1)
 
@@ -274,7 +278,7 @@
                 parts[source, b] = zero
 
 
-    def prepare(source, low, high):
+    def prepare(source, low, high, single=False):
         @pl.loop(low, high)
         def _(e):
             at_row = place * rows + e - outer + owned
@@ -295,7 +299,7 @@
                     from_slot = from_slot + jnp.where(ranks[k] == s, k, 0)
                     at = at + jnp.where(ranks[k] == s, column[k], 0)
                 order[e, s] = jnp.clip(at + move, 0, rows + 2 * reach - 1)
-                high_part, low_part = split(source[e - low, from_slot].T)
+                high_part, low_part = split((source[from_slot] if single else source[e - low, from_slot]).T)
                 weights[e, s * LANES:(s + 1) * LANES, 0:LANES] = high_part
                 weights[e, s * LANES:(s + 1) * LANES, LANES:2 * LANES] = low_part
 
@@ -314,15 +318,27 @@
     own_blocks.wait()
     prepare(raw_own, outer, outer + rows)
 
+    def prepare_most(side):
+        at = side * (outer + rows)
+        prepare(raw_right if side else raw_left, at, at + most)
+
+    def prepare_last(side):
+        at = side * (outer + rows) + most
+        prepare(raw_last[side], at, at + 1, single=True)
+
+    def prepare_beside(side):
+        for copy in beside(side):
+            copy.wait()
+        prepare_most(side)
+        prepare_last(side)
+
     @pl.when(place > 0)
     def _():
-        left_blocks.wait()
-        prepare(raw_left, 0, outer)
+        prepare_beside(0)
 
     @pl.when(place < FOLDS - 1)
     def _():
-        right_blocks.wait()
-        prepare(raw_right, outer + rows, wide)
+        prepare_beside(1)
 
     @pl.when(jnp.logical_not(has_left))
     def _():
@@ -353,48 +369,58 @@
         iterate[b] = zero
         store_vector(0, reach + b, begun)
 
-    def exchange(parity):
-        def copy(source, target, side, which):
-            return pltpu.make_async_remote_copy(
-                src_ref=source, dst_ref=target,
-                send_sem=h_send.at[parity, side, which], recv_sem=h_recv.at[parity, 1 - side, which],
-                device_id=right if side else left, device_id_type=MESH,
-            )
-
-        return [
-            [
-                copy(update.at[parity, pl.ds(0, reach)], halo_update.at[parity, 1], 0, 0),
-                copy(resid.at[parity, pl.ds(0, outer)], halo_resid.at[parity, 1], 0, 1),
-            ],
-            [
-                copy(update.at[parity, pl.ds(rows - reach, reach)], halo_update.at[parity, 0], 1, 0),
-                copy(resid.at[parity, pl.ds(rows - outer, outer)], halo_resid.at[parity, 0], 1, 1),
-            ],
-        ]
-
-    def send(parity):
-        copies = exchange(parity)
-        for which in range(2):
-            @pl.when(has_left)
+    NEAR, REST = [0], [1, 2]
+
+    def exchange(parity, side, which):
+        source, target, length, near, into = [
+            (update, halo_update, HB, 0, reach - HB), (resid, halo_resid, outer, 0, 0), (update, halo_update, reach - HB, HB, 0),
+        ][which]
+        if side:
+            source_at, target_at = rows - near - length, into
+        else:
+            source_at, target_at = near, near
+        return pltpu.make_async_remote_copy(
+            src_ref=source.at[parity, pl.ds(source_at, length)],
+            dst_ref=target.at[parity, 1 - side, pl.ds(target_at, length)],
+            send_sem=h_send.at[parity, side, which], recv_sem=h_recv.at[parity, 1 - side, which],
+            device_id=right if side else left, device_id_type=MESH,
+        )
+
+    inner_right = jnp.logical_and(has_right, place < FOLDS - 1)
+
+    def send(parity, chosen):
+        @pl.when(right_edge)
+        def _():
+            for which in chosen:
+                exchange(parity, 1, which).start()
+
+        @pl.when(has_left)
+        def _():
+            for which in chosen:
+                exchange(parity, 0, which).start()
+
+        @pl.when(inner_right)
+        def _():
+            for which in chosen:
+                exchange(parity, 1, which).start()
+
+    def sent_all(parity):
+        for side, there in enumerate((has_left, has_right)):
+            @pl.when(there)
             def _():
-                copies[0][which].start()
-
-            @pl.when(has_right)
+                for which in NEAR + REST:
+                    exchange(parity, side, which).wait_send()
+
+    def receive(parity, chosen):
+        for side, there in enumerate((has_left, has_right)):
+            @pl.when(there)
             def _():
-                copies[1][which].start()
-
-    def receive(parity, which):
-        copies = exchange(parity)
-
-        @pl.when(has_left)
-        def _():
-            copies[1][which].wait_recv()
-
-        @pl.when(has_right)
-        def _():
-            copies[0][which].wait_recv()
-
-    send(0)
+                for which in chosen:
+                    exchange(parity, 1 - side, which).wait_recv()
+
+    send(0, NEAR)
+    send(0, REST)
+    edge_start(3, 4)
 
     for other in range(1, FOLDS):
         @pl.when(reachable(chip, position_of((fold + other) % FOLDS)))
@@ -402,17 +428,20 @@
             message(other)[1].wait_send()
 
 
-    def edge_done(side):
-        arrived = (edge_left if side else edge_right)()
+    def edge_most(side):
+        arrived = edge(1 - side)
         arrived[0].wait_recv()
-        into = pltpu.make_async_copy(
-            edge_columns.at[side], all_columns.at[2 * side], column_sem.at[1 + side]
-        )
+        into = pltpu.make_async_copy(edge_columns.at[side], all_columns.at[2 * side], column_sem.at[1 + side])
         into.start()
         into.wait()
         arrived[1].wait_recv()
-        prepare(raw_right if side else raw_left, side * (outer + rows), side * (outer + rows) + outer)
-        for copy in (edge_right if side else edge_left)():
+        prepare_most(side)
+
+    def edge_last(side):
+        for copy in edge(1 - side)[2:]:
+            copy.wait_recv()
+        prepare_last(side)
+        for copy in edge(side):
             copy.wait_send()
 
     def product(which, e, low, high):
@@ -463,8 +492,16 @@
 
             margin = HB * (depth - 1 - level)
             if level > 0:
-                for e in range(outer - margin, outer + rows + margin):
-                    finish(e, product(now, e, 0, KB))
+                ends = list(range(HB)) + list(range(rows - HB, rows))
+                for j in ends:
+                    finish(j + outer, product(now, j + outer, 0, KB))
+
+                @pl.when(turn + 1 < rounds)
+                def _():
+                    send(1 - parity, NEAR)
+
+                for j in range(HB, rows - HB):
+                    finish(j + outer, product(now, j + outer, 0, KB))
                 continue
 
             for j in range(rows):
@@ -474,9 +511,17 @@
                     finish(j + outer, applied)
                 else:
                     partial[j] = applied
-            receive(parity, 0)
-            for b in range(reach):
-                store_vector(now, b, halo_update[parity, 0, b])
+
+            def first_turn(there, act, side):
+                @pl.when(jnp.logical_and(turn == 0, there))
+                def _():
+                    act(side)
+
+            first_turn(left_edge, edge_most, 0)
+            first_turn(right_edge, edge_most, 1)
+            receive(parity, NEAR)
+            for b in range(HB):
+                store_vector(now, reach - HB + b, halo_update[parity, 0, reach - HB + b])
                 store_vector(now, reach + rows + b, halo_update[parity, 1, b])
             for j in range(rows):
                 low, high = own_slots(j)
@@ -484,32 +529,19 @@
                     finish(j + outer, partial[j] + product(now, j + outer, 0, low))
                 elif high < KB:
                     finish(j + outer, partial[j] + product(now, j + outer, high, KB))
-            receive(parity, 1)
-
-            @pl.when(jnp.logical_and(turn == 0, left_edge))
-            def _():
-                edge_done(0)
-
-            @pl.when(jnp.logical_and(turn == 0, right_edge))
-            def _():
-                edge_done(1)
-
+            receive(parity, REST)
+            for b in range(reach - HB):
+                store_vector(now, b, halo_update[parity, 0, b])
+                store_vector(now, reach + rows + HB + b, halo_update[parity, 1, HB + b])
+            first_turn(left_edge, edge_last, 0)
+            first_turn(right_edge, edge_last, 1)
             for e in list(range(outer)) + list(range(outer + rows, wide)):
                 finish(e, product(now, e, 0, KB))
-
-        copies = exchange(parity)
-        for which in range(2):
-            @pl.when(has_left)
-            def _():
-                copies[0][which].wait_send()
-
-            @pl.when(has_right)
-            def _():
-                copies[1][which].wait_send()
+            sent_all(parity)
 
         @pl.when(turn + 1 < rounds)
         def _():
-            send(1 - parity)
+            send(1 - parity, REST)
 
     for b in range(rows):
         gathered[place * rows + b] = iterate[b] + update[rounds % 2, b]
@@ -579,8 +611,10 @@
             vectors(owned),
             vectors(folds, rows),
             pltpu.VMEM((rows, KB, LANES, LANES), f32),
-            pltpu.VMEM((outer, KB, LANES, LANES), f32),
-            pltpu.VMEM((outer, KB, LANES, LANES), f32),
+            pltpu.VMEM((outer - 1, KB, LANES, LANES), f32),
+            pltpu.VMEM((outer - 1, KB, LANES, LANES), f32),
+            pltpu.VMEM((KB, LANES, LANES), f32),
+            pltpu.VMEM((KB, LANES, LANES), f32),
             pltpu.VMEM((rows + 2 * outer, KB * LANES, 2 * LANES), jnp.bfloat16),
             pltpu.SMEM((rows + 2 * outer, KB), i32),
             pltpu.SMEM((3, KB, owned), i32),
@@ -596,8 +630,8 @@
             vectors(2, 2, reach),
             vectors(2, 2, outer),
             vectors(owned),
-            dma((4,)), dma((4,)), dma((2, 2)), dma((2, 2)), dma, dma, dma((8,)), dma((8,)),
-            dma((2, 2, 2)), dma((2, 2, 2)), dma((7,)), dma((8,)),
+            dma((6,)), dma((4,)), dma((4, 2)), dma((4, 2)), dma, dma, dma((8,)), dma((8,)),
+            dma((2, 2, 3)), dma((2, 2, 3)), dma((7,)), dma((8,)),
         ],
         compiler_params=pltpu.CompilerParams(collective_id=0, has_side_effects=True),
     )(counts, columns.T, right_side, initial, blocks)

time: 55.7 us -> 54.7 us (0.982)
  Pallas kernels: 54 us -> 53 us
    pallas_call x1, Pallas kernels: 54 us -> 53 us  [on_device(): pl.pallas_call(functools.partial(kernel, rows, groups, depth), out_shape=...]
where the time goes in v4:
time: 54.7 us; the launch traced here: 54.6 us
  Pallas kernels  53 us (97%)
  local copies, waits for them, and re-layouts  1.57 us (3%)
    pallas_call x1, Pallas kernels, on_device(): pl.pallas_call(functools.partial(kernel, rows, groups, depth), out_shape=...  53 us
    unnamed x1, local copies, waits for them, and re-layouts  1.57 us

profile of v4, /device:TPU:25, one launch (start us, length us, event | category | flops | bytes accessed | tf_op | source)
XLA Modules:
  0.0 54.6 jit_solution(8406864186869555988)
XLA Ops:
  0.0 53.0 %shard_map.55 = f32[16,2048]{1,0:T(8,128)} custom-call(s32[1,8]{1,0:T(1,128)} %counts_in.1, s32[5,64]{1,0:T(8,128)} %bitcast.1, f32[16,2048]{1,0:T(8,128)} %right_side.1, f32[16,2048]{1,0:T(8,128)} %initial.1, f32[64,5,128,128]{3,2,1,0:T(8,128)} %blocks.1), custom_call_target="tpu_custom_call" | custom-call | tf_op jit(solution)/shard_map/pallas_call | solution.py:601
  53.0 1.6 %copy.7 = f32[16,2048]{1,0:T(8,128)} copy(f32[16,2048]{1,0:T(8,128)} %shard_map.55) | data formatting | bytes 262144

commit v5 on v4

--- a/solution.py
+++ b/solution.py
@@ -17,7 +17,7 @@
 FOLDS = 8
 CHIPS = 4
 DEPTH = 2
-EARLY = 2
+EARLY = 4
 
 upper_bound = 4.5
 lower_bound = 1.35
@@ -75,8 +75,8 @@
     last = groups * FOLDS - 1
     has_left, has_right = rank > 0, rank < last
     left_edge, right_edge = jnp.logical_and(place == 0, has_left), jnp.logical_and(place == FOLDS - 1, has_right)
-    left = {"group": group - (7 - place) // 7, "fold": fold_of((place + 7) % 8)}
-    right = {"group": group + place // 7, "fold": fold_of((place + 1) % 8)}
+    left = {"group": (group + groups - (7 - place) // 7) % groups, "fold": fold_of((place + 7) % 8)}
+    right = {"group": (group + place // 7) % groups, "fold": fold_of((place + 1) % 8)}
 
     own_blocks = pltpu.make_async_copy(
         blocks.at[pl.ds(place * rows, rows)], raw_own, block_sem.at[0]
@@ -95,11 +95,11 @@
 
     own_columns = pltpu.make_async_copy(columns, all_columns.at[1], column_sem.at[0])
     barrier = pltpu.get_barrier_semaphore()
-    @pl.when(left_edge)
+    @pl.when(place == 0)
     def _():
         pl.semaphore_signal(barrier, inc=1, device_id=left, device_id_type=MESH)
 
-    @pl.when(right_edge)
+    @pl.when(place == FOLDS - 1)
     def _():
         pl.semaphore_signal(barrier, inc=1, device_id=right, device_id_type=MESH)
 
@@ -133,8 +133,7 @@
         for copy in beside(1):
             copy.start()
 
-    outside = (7 - place) // 7 * ((rank + last) // (last + 1)) + place // 7 * (1 - (rank + 1) // (last + 1))
-    pl.semaphore_wait(barrier, FOLDS - 1 + outside)
+    pl.semaphore_wait(barrier, FOLDS - 1 + (7 - place) // 7 + place // 7)
 
     def swap(source):
         return pltpu.make_async_remote_copy(
@@ -303,16 +302,11 @@
                 weights[e, s * LANES:(s + 1) * LANES, 0:LANES] = high_part
                 weights[e, s * LANES:(s + 1) * LANES, LANES:2 * LANES] = low_part
 
-    def absent(low, side):
+    def absent(low):
         for e in range(low, low + outer):
             for s in range(KB):
                 order[e, s] = 0
             weights[e] = jnp.zeros((KB * LANES, 2 * LANES), jnp.bfloat16)
-        for parity in range(2):
-            for b in range(reach):
-                halo_update[parity, side, b] = zero
-            for b in range(outer):
-                halo_resid[parity, side, b] = zero
 
     own_columns.wait()
     own_blocks.wait()
@@ -342,11 +336,11 @@
 
     @pl.when(jnp.logical_not(has_left))
     def _():
-        absent(0, 0)
+        absent(0)
 
     @pl.when(jnp.logical_not(has_right))
     def _():
-        absent(outer + rows, 1)
+        absent(outer + rows)
 
     vectors = [vector_even, vector_odd]
 
@@ -372,51 +366,36 @@
     NEAR, REST = [0], [1, 2]
 
     def exchange(parity, side, which):
-        source, target, length, near, into = [
-            (update, halo_update, HB, 0, reach - HB), (resid, halo_resid, outer, 0, 0), (update, halo_update, reach - HB, HB, 0),
+        source, target, length, near = [
+            (update, halo_update, HB, 0), (resid, halo_resid, outer, 0), (update, halo_update, reach - HB, HB),
         ][which]
-        if side:
-            source_at, target_at = rows - near - length, into
-        else:
-            source_at, target_at = near, near
+        mirrored = source is update
         return pltpu.make_async_remote_copy(
-            src_ref=source.at[parity, pl.ds(source_at, length)],
-            dst_ref=target.at[parity, 1 - side, pl.ds(target_at, length)],
+            src_ref=source.at[parity, pl.ds(near + side * (rows - 2 * near - length), length)],
+            dst_ref=target.at[parity, 1 - side, pl.ds(near + side * (reach - 2 * near - length if mirrored else 0), length)],
             send_sem=h_send.at[parity, side, which], recv_sem=h_recv.at[parity, 1 - side, which],
-            device_id=right if side else left, device_id_type=MESH,
+            device_id={name: left[name] + side * (right[name] - left[name]) for name in left}, device_id_type=MESH,
         )
 
-    inner_right = jnp.logical_and(has_right, place < FOLDS - 1)
+    sides = [place // 7, 1 - place // 7]
 
     def send(parity, chosen):
-        @pl.when(right_edge)
-        def _():
-            for which in chosen:
-                exchange(parity, 1, which).start()
-
-        @pl.when(has_left)
-        def _():
-            for which in chosen:
-                exchange(parity, 0, which).start()
-
-        @pl.when(inner_right)
-        def _():
-            for which in chosen:
-                exchange(parity, 1, which).start()
+        for which in chosen:
+            for side in sides:
+                exchange(parity, side, which).start()
 
     def sent_all(parity):
-        for side, there in enumerate((has_left, has_right)):
-            @pl.when(there)
-            def _():
-                for which in NEAR + REST:
-                    exchange(parity, side, which).wait_send()
+        for which in NEAR + REST:
+            for side in range(2):
+                exchange(parity, side, which).wait_send()
 
     def receive(parity, chosen):
-        for side, there in enumerate((has_left, has_right)):
-            @pl.when(there)
-            def _():
-                for which in chosen:
-                    exchange(parity, 1 - side, which).wait_recv()
+        for which in chosen:
+            for side in range(2):
+                exchange(parity, 1 - side, which).wait_recv()
+
+    def halo_of(ref, parity, side, b):
+        return jnp.where(has_right if side else has_left, ref[parity, side, b], 0.0)
 
     send(0, NEAR)
     send(0, REST)
@@ -455,10 +434,7 @@
     keeps, gains = step_factors()
     rounds = SWEEPS * DEGREE // depth
 
-    @pl.loop(0, rounds)
-    def _(turn):
-        parity = turn % 2
-
+    def one_turn(turn, parity, first_turn, last_turn):
         for level in range(depth):
             now, later = level % 2, (level + 1) % 2
             keep, gain = jnp.float32(keeps[level]), jnp.float32(gains[level])
@@ -475,9 +451,9 @@
                 elif inside:
                     old, left_over = update[parity, own], resid[parity, own]
                 elif own < 0:
-                    old, left_over = halo_update[parity, 0, e + HB], halo_resid[parity, 0, e]
+                    old, left_over = halo_of(halo_update, parity, 0, e + HB), halo_of(halo_resid, parity, 0, e)
                 else:
-                    old, left_over = halo_update[parity, 1, own - rows], halo_resid[parity, 1, own - rows]
+                    old, left_over = halo_of(halo_update, parity, 1, own - rows), halo_of(halo_resid, parity, 1, own - rows)
                 left_over = left_over - applied
                 fresh = keep * old + gain * left_over
                 if inside:
@@ -496,10 +472,8 @@
                 for j in ends:
                     finish(j + outer, product(now, j + outer, 0, KB))
 
-                @pl.when(turn + 1 < rounds)
-                def _():
+                if not last_turn:
                     send(1 - parity, NEAR)
-
                 for j in range(HB, rows - HB):
                     finish(j + outer, product(now, j + outer, 0, KB))
                 continue
@@ -512,17 +486,13 @@
                 else:
                     partial[j] = applied
 
-            def first_turn(there, act, side):
-                @pl.when(jnp.logical_and(turn == 0, there))
-                def _():
-                    act(side)
-
-            first_turn(left_edge, edge_most, 0)
-            first_turn(right_edge, edge_most, 1)
+            if first_turn:
+                at_edges(edge_most)
+            sent_all(parity)
             receive(parity, NEAR)
             for b in range(HB):
-                store_vector(now, reach - HB + b, halo_update[parity, 0, reach - HB + b])
-                store_vector(now, reach + rows + b, halo_update[parity, 1, b])
+                store_vector(now, reach - HB + b, halo_of(halo_update, parity, 0, reach - HB + b))
+                store_vector(now, reach + rows + b, halo_of(halo_update, parity, 1, b))
             for j in range(rows):
                 low, high = own_slots(j)
                 if low > 0:
@@ -531,17 +501,32 @@
                     finish(j + outer, partial[j] + product(now, j + outer, high, KB))
             receive(parity, REST)
             for b in range(reach - HB):
-                store_vector(now, b, halo_update[parity, 0, b])
-                store_vector(now, reach + rows + HB + b, halo_update[parity, 1, HB + b])
-            first_turn(left_edge, edge_last, 0)
-            first_turn(right_edge, edge_last, 1)
+                store_vector(now, b, halo_of(halo_update, parity, 0, b))
+                store_vector(now, reach + rows + HB + b, halo_of(halo_update, parity, 1, HB + b))
+            if first_turn:
+                at_edges(edge_last)
             for e in list(range(outer)) + list(range(outer + rows, wide)):
                 finish(e, product(now, e, 0, KB))
-            sent_all(parity)
-
-        @pl.when(turn + 1 < rounds)
-        def _():
+
+        if not last_turn:
             send(1 - parity, REST)
+
+    def at_edges(act):
+        @pl.when(left_edge)
+        def _():
+            act(0)
+
+        @pl.when(right_edge)
+        def _():
+            act(1)
+
+    one_turn(0, 0, True, False)
+
+    @pl.loop(1, rounds - 1)
+    def _(turn):
+        one_turn(turn, turn % 2, False, False)
+
+    one_turn(rounds - 1, (rounds - 1) % 2, False, True)
 
     for b in range(rows):
         gathered[place * rows + b] = iterate[b] + update[rounds % 2, b]

time: 54.7 us -> 56.9 us (1.040)
  the two profiles are of different devices: /device:TPU:25 before, /device:TPU:1 now
where the time goes in v5:
time: 56.9 us; the launch traced here: 56.7 us
  Pallas kernels  55.2 us (97%)
  local copies, waits for them, and re-layouts  1.57 us (3%)
    pallas_call x1, Pallas kernels, on_device(): pl.pallas_call(functools.partial(kernel, rows, groups, depth), out_shape=...  55.2 us
    unnamed x1, local copies, waits for them, and re-layouts  1.57 us

profile of v5, /device:TPU:1, one launch (start us, length us, event | category | flops | bytes accessed | tf_op | source)
XLA Modules:
  0.0 56.7 jit_solution(3671267947835136562)
XLA Ops:
  0.0 55.2 %shard_map.55 = f32[16,2048]{1,0:T(8,128)} custom-call(s32[1,8]{1,0:T(1,128)} %counts_in.1, s32[5,64]{1,0:T(8,128)} %bitcast.1, f32[16,2048]{1,0:T(8,128)} %right_side.1, f32[16,2048]{1,0:T(8,128)} %initial.1, f32[64,5,128,128]{3,2,1,0:T(8,128)} %blocks.1), custom_call_target="tpu_custom_call" | custom-call | tf_op jit(solution)/shard_map/pallas_call | solution.py:586
  55.2 1.6 %copy.7 = f32[16,2048]{1,0:T(8,128)} copy(f32[16,2048]{1,0:T(8,128)} %shard_map.55) | data formatting | bytes 262144

commit v6 on v5

--- a/solution.py
+++ b/solution.py
@@ -43,14 +43,11 @@
 
 
 def position_of(fold):
-    chip, core = fold // 2, fold % 2
-    return chip + core * (7 - 2 * chip)
+    return (fold + 7) % 8
 
 
 def fold_of(position):
-    core = position // 4
-    chip = position + core * (7 - 2 * position)
-    return 2 * chip + core
+    return (position + 1) % 8
 
 
 def kernel(
@@ -95,11 +92,11 @@
 
     own_columns = pltpu.make_async_copy(columns, all_columns.at[1], column_sem.at[0])
     barrier = pltpu.get_barrier_semaphore()
-    @pl.when(place == 0)
+    @pl.when(left_edge)
     def _():
         pl.semaphore_signal(barrier, inc=1, device_id=left, device_id_type=MESH)
 
-    @pl.when(place == FOLDS - 1)
+    @pl.when(right_edge)
     def _():
         pl.semaphore_signal(barrier, inc=1, device_id=right, device_id_type=MESH)
 
@@ -133,7 +130,8 @@
         for copy in beside(1):
             copy.start()
 
-    pl.semaphore_wait(barrier, FOLDS - 1 + (7 - place) // 7 + place // 7)
+    outside = (7 - place) // 7 * ((rank + last) // (last + 1)) + place // 7 * (1 - (rank + 1) // (last + 1))
+    pl.semaphore_wait(barrier, FOLDS - 1 + outside)
 
     def swap(source):
         return pltpu.make_async_remote_copy(
@@ -363,11 +361,11 @@
         iterate[b] = zero
         store_vector(0, reach + b, begun)
 
-    NEAR, REST = [0], [1, 2]
+    NEAR, FAR, RESID = [0], [1], [2]
 
     def exchange(parity, side, which):
         source, target, length, near = [
-            (update, halo_update, HB, 0), (resid, halo_resid, outer, 0), (update, halo_update, reach - HB, HB),
+            (update, halo_update, HB, 0), (update, halo_update, reach - HB, HB), (resid, halo_resid, outer, 0),
         ][which]
         mirrored = source is update
         return pltpu.make_async_remote_copy(
@@ -377,28 +375,49 @@
             device_id={name: left[name] + side * (right[name] - left[name]) for name in left}, device_id_type=MESH,
         )
 
-    sides = [place // 7, 1 - place // 7]
+    inside = jnp.logical_and(has_left, has_right)
+
+    def neighbours(act):
+        @pl.when(inside)
+        def _():
+            act(range(2))
+
+        @pl.when(jnp.logical_not(has_left))
+        def _():
+            act([1])
+
+        @pl.when(jnp.logical_not(has_right))
+        def _():
+            act([0])
 
     def send(parity, chosen):
-        for which in chosen:
-            for side in sides:
-                exchange(parity, side, which).start()
-
-    def sent_all(parity):
-        for which in NEAR + REST:
-            for side in range(2):
-                exchange(parity, side, which).wait_send()
+        def act(sides):
+            for which in chosen:
+                for side in sides:
+                    exchange(parity, side, which).start()
+
+        neighbours(act)
+
+    def sent_all(parity, chosen):
+        def act(sides):
+            for which in chosen:
+                for side in sides:
+                    exchange(parity, side, which).wait_send()
+
+        neighbours(act)
 
     def receive(parity, chosen):
-        for which in chosen:
-            for side in range(2):
-                exchange(parity, 1 - side, which).wait_recv()
+        def act(sides):
+            for which in chosen:
+                for side in sides:
+                    exchange(parity, 1 - side, which).wait_recv()
+
+        neighbours(act)
 
     def halo_of(ref, parity, side, b):
         return jnp.where(has_right if side else has_left, ref[parity, side, b], 0.0)
 
-    send(0, NEAR)
-    send(0, REST)
+    send(0, NEAR + FAR + RESID)
     edge_start(3, 4)
 
     for other in range(1, FOLDS):
@@ -434,14 +453,12 @@
     keeps, gains = step_factors()
     rounds = SWEEPS * DEGREE // depth
 
-    def one_turn(turn, parity, first_turn, last_turn):
+    def one_turn(turn, first_turn=False, last_turn=False):
+        parity, phase = turn % 2, turn % (DEGREE // depth)
+        given = RESID if first_turn else []
         for level in range(depth):
             now, later = level % 2, (level + 1) % 2
-            keep, gain = jnp.float32(keeps[level]), jnp.float32(gains[level])
-            for phase in range(1, DEGREE // depth):
-                chosen = turn % (DEGREE // depth) == phase
-                keep = jnp.where(chosen, jnp.float32(keeps[phase * depth + level]), keep)
-                gain = jnp.where(chosen, jnp.float32(gains[phase * depth + level]), gain)
+            keep, gain = keeps[phase * depth + level], gains[phase * depth + level]
 
             def finish(e, applied):
                 own = e - outer
@@ -450,10 +467,14 @@
                     old, left_over = mid_update[e], mid_resid[e]
                 elif inside:
                     old, left_over = update[parity, own], resid[parity, own]
-                elif own < 0:
-                    old, left_over = halo_of(halo_update, parity, 0, e + HB), halo_of(halo_resid, parity, 0, e)
                 else:
-                    old, left_over = halo_of(halo_update, parity, 1, own - rows), halo_of(halo_resid, parity, 1, own - rows)
+                    side, at = (0, e + HB) if own < 0 else (1, own - rows)
+                    old = halo_of(halo_update, parity, side, at)
+                    if first_turn:
+                        left_over = halo_of(halo_resid, parity, side, at - (1 - side) * HB)
+                    else:
+                        before = (phase * depth + DEGREE - 1) % DEGREE
+                        left_over = (old - keeps[before] * mid_update[e]) * (1.0 / gains[before])
                 left_over = left_over - applied
                 fresh = keep * old + gain * left_over
                 if inside:
@@ -488,7 +509,7 @@
 
             if first_turn:
                 at_edges(edge_most)
-            sent_all(parity)
+            sent_all(parity, NEAR + FAR + given)
             receive(parity, NEAR)
             for b in range(HB):
                 store_vector(now, reach - HB + b, halo_of(halo_update, parity, 0, reach - HB + b))
@@ -499,7 +520,7 @@
                     finish(j + outer, partial[j] + product(now, j + outer, 0, low))
                 elif high < KB:
                     finish(j + outer, partial[j] + product(now, j + outer, high, KB))
-            receive(parity, REST)
+            receive(parity, FAR + given)
             for b in range(reach - HB):
                 store_vector(now, b, halo_of(halo_update, parity, 0, b))
                 store_vector(now, reach + rows + HB + b, halo_of(halo_update, parity, 1, HB + b))
@@ -509,7 +530,7 @@
                 finish(e, product(now, e, 0, KB))
 
         if not last_turn:
-            send(1 - parity, REST)
+            send(1 - parity, FAR)
 
     def at_edges(act):
         @pl.when(left_edge)
@@ -520,13 +541,14 @@
         def _():
             act(1)
 
-    one_turn(0, 0, True, False)
-
-    @pl.loop(1, rounds - 1)
-    def _(turn):
-        one_turn(turn, turn % 2, False, False)
-
-    one_turn(rounds - 1, (rounds - 1) % 2, False, True)
+    one_turn(0, first_turn=True)
+
+    @pl.loop(0, (rounds - 2) // 2)
+    def _(_):
+        one_turn(1)
+        one_turn(2)
+
+    one_turn(rounds - 1, last_turn=True)
 
     for b in range(rows):
         gathered[place * rows + b] = iterate[b] + update[rounds % 2, b]
@@ -538,16 +560,25 @@
             device_id={"group": group, "fold": dest}, device_id_type=MESH,
         )
 
+    def wanted(where, dest, act):
+        @pl.when(reachable(dest // 2, where))
+        def _():
+            act()
+
+    def forward(where, which):
+        piece(where, partner, 0).wait_recv()
+        piece(where, partner, which).start()
+
     for other in (2, 1, 3):
-        piece(place, (fold + 2 * other) % FOLDS, other).start()
-    piece(place, partner, 0).start()
+        dest = (fold + 2 * other) % FOLDS
+        wanted(place, dest, piece(place, dest, other).start)
+    wanted(place, partner, piece(place, partner, 0).start)
     for other in (1, 3, 2):
         where = position_of((fold + 2 * other) % FOLDS)
-        piece(where, partner, 0).wait_recv()
-        piece(where, partner, 3 + other).start()
+        wanted(where, partner, functools.partial(forward, where, 3 + other))
     for other in range(CHIPS):
         where = position_of((partner + 2 * other) % FOLDS)
-        piece(where, partner, 0).wait_recv()
+        wanted(where, fold, piece(where, partner, 0).wait_recv)
 
     begin, live = start_of(fold), count_of(fold)
     shift = begin & (LANES - 1)
@@ -564,8 +595,10 @@
         out[:, m * LANES:(m + 1) * LANES] = jnp.where(lane + m * LANES < live, value, 0.0)
         here = after
 
-    for which in range(7):
-        piece(place, partner, which).wait_send()
+    for other in range(CHIPS):
+        wanted(place, (fold + 2 * other) % FOLDS if other else partner, piece(place, partner, other).wait_send)
+        if other:
+            wanted(position_of((fold + 2 * other) % FOLDS), partner, piece(place, partner, 3 + other).wait_send)
 
 
 def on_device(right_side, initial, counts, columns, blocks):

time: 56.9 us -> 51.5 us (0.905)
  the two profiles are of different devices: /device:TPU:1 before, /device:TPU:25 now
where the time goes in v6:
time: 51.5 us; the launch traced here: 51.3 us
  Pallas kernels  49.8 us (97%)
  local copies, waits for them, and re-layouts  1.57 us (3%)
    pallas_call x1, Pallas kernels, on_device(): pl.pallas_call(functools.partial(kernel, rows, groups, depth), out_shape=...  49.8 us
    unnamed x1, local copies, waits for them, and re-layouts  1.57 us

profile of v6, /device:TPU:25, one launch (start us, length us, event | category | flops | bytes accessed | tf_op | source)
XLA Modules:
  0.0 51.3 jit_solution(17867740746861076339)
XLA Ops:
  0.0 49.8 %shard_map.55 = f32[16,2048]{1,0:T(8,128)} custom-call(s32[1,8]{1,0:T(1,128)} %counts_in.1, s32[5,64]{1,0:T(8,128)} %bitcast.1, f32[16,2048]{1,0:T(8,128)} %right_side.1, f32[16,2048]{1,0:T(8,128)} %initial.1, f32[64,5,128,128]{3,2,1,0:T(8,128)} %blocks.1), custom_call_target="tpu_custom_call" | custom-call | tf_op jit(solution)/shard_map/pallas_call | solution.py:619
  49.8 1.6 %copy.7 = f32[16,2048]{1,0:T(8,128)} copy(f32[16,2048]{1,0:T(8,128)} %shard_map.55) | data formatting | bytes 262144

commit v7 on v6

--- a/solution.py
+++ b/solution.py
@@ -17,7 +17,7 @@
 FOLDS = 8
 CHIPS = 4
 DEPTH = 2
-EARLY = 4
+RELAYS = (2, 6)
 
 upper_bound = 4.5
 lower_bound = 1.35
@@ -53,9 +53,9 @@
 def kernel(
     rows, groups, depth,
     counts_in, columns, right_side, initial, blocks, out,
-    counts, mine, raw, aligned, sent, parts, raw_own, raw_left, raw_right, left_last, right_last, weights, order, all_columns, edge_columns,
+    counts, mine, raw, aligned, sent, parts, raw_own, raw_left, raw_right, left_last, right_last, handed, weights, order, all_columns, edge_columns,
     vector_even, vector_odd, update, resid, mid_update, mid_resid, iterate, partial, halo_update, halo_resid, gathered,
-    block_sem, column_sem, edge_send, edge_recv, a_send, a_recv, b_send, b_recv, h_send, h_recv, c_send, c_recv,
+    block_sem, column_sem, edge_send, edge_recv, relay_sems, last_sem, a_send, a_recv, b_send, b_recv, h_send, h_recv, c_send, c_recv,
 ):
     group, fold = lax.axis_index("group"), lax.axis_index("fold")
     chip, core = fold // 2, fold % 2
@@ -71,6 +71,9 @@
     rank = group * FOLDS + place
     last = groups * FOLDS - 1
     has_left, has_right = rank > 0, rank < last
+    relay_left, relay_right = fold == RELAYS[0], fold == RELAYS[1]
+    relay = jnp.logical_or(relay_left, relay_right)
+    below, above = {"group": (group + groups - 1) % groups, "fold": fold}, {"group": (group + 1) % groups, "fold": fold}
     left_edge, right_edge = jnp.logical_and(place == 0, has_left), jnp.logical_and(place == FOLDS - 1, has_right)
     left = {"group": (group + groups - (7 - place) // 7) % groups, "fold": fold_of((place + 7) % 8)}
     right = {"group": (group + place // 7) % groups, "fold": fold_of((place + 1) % 8)}
@@ -100,6 +103,14 @@
     def _():
         pl.semaphore_signal(barrier, inc=1, device_id=right, device_id_type=MESH)
 
+    @pl.when(jnp.logical_and(relay, group > 0))
+    def _():
+        pl.semaphore_signal(barrier, inc=1, device_id=below, device_id_type=MESH)
+
+    @pl.when(jnp.logical_and(relay, group < groups - 1))
+    def _():
+        pl.semaphore_signal(barrier, inc=1, device_id=above, device_id_type=MESH)
+
     for other in (4, 3, 5, 2, 6, 1, 7):
         pl.semaphore_signal(barrier, inc=1, device_id={"group": group, "fold": (fold + other) % FOLDS}, device_id_type=MESH)
 
@@ -131,7 +142,9 @@
             copy.start()
 
     outside = (7 - place) // 7 * ((rank + last) // (last + 1)) + place // 7 * (1 - (rank + 1) // (last + 1))
-    pl.semaphore_wait(barrier, FOLDS - 1 + outside)
+    is_relay = jnp.where(relay, 1, 0)
+    beyond = is_relay * ((group + groups - 1) // groups + 1 - (group + 1) // groups)
+    pl.semaphore_wait(barrier, FOLDS - 1 + outside + beyond)
 
     def swap(source):
         return pltpu.make_async_remote_copy(
@@ -153,8 +166,6 @@
         refs = [
             (columns, edge_columns.at[target]),
             (blocks.at[pl.ds(begin, most)], (raw_right if target else raw_left)),
-            (blocks.at[begin + most, pl.ds(0, EARLY)], raw_last[target].at[pl.ds(0, EARLY)]),
-            (blocks.at[begin + most, pl.ds(EARLY, KB - EARLY)], raw_last[target].at[pl.ds(EARLY, KB - EARLY)]),
         ]
         return [
             pltpu.make_async_remote_copy(
@@ -164,18 +175,35 @@
             for i, (source, dest) in enumerate(refs)
         ]
 
-    def edge_start(low, high):
-        @pl.when(left_edge)
-        def _():
-            for copy in edge(0)[low:high]:
-                copy.start()
-
-        @pl.when(right_edge)
-        def _():
-            for copy in edge(1)[low:high]:
-                copy.start()
-
-    edge_start(0, 3)
+    def relay_in(side):
+        return pltpu.make_async_remote_copy(
+            src_ref=blocks.at[(owned - outer if side else 0) + most], dst_ref=handed, send_sem=relay_sems.at[0],
+            recv_sem=relay_sems.at[1], device_id=above if side else below, device_id_type=MESH,
+        )
+
+    def relay_out(side):
+        return pltpu.make_async_remote_copy(
+            src_ref=handed, dst_ref=raw_last[side], send_sem=relay_sems.at[2], recv_sem=last_sem.at[side],
+            device_id={"group": group, "fold": fold_of(side * (FOLDS - 1))}, device_id_type=MESH,
+        )
+
+    @pl.when(left_edge)
+    def _():
+        for copy in edge(0):
+            copy.start()
+
+    @pl.when(right_edge)
+    def _():
+        for copy in edge(1):
+            copy.start()
+
+    @pl.when(jnp.logical_and(relay_left, group < groups - 1))
+    def _():
+        relay_in(1).start()
+
+    @pl.when(jnp.logical_and(relay_right, group > 0))
+    def _():
+        relay_in(0).start()
 
     lane = lax.broadcasted_iota(jnp.int32, (NV, LANES), 1)
 
@@ -347,6 +375,16 @@
         vectors[which][index, 0:NV] = high
         vectors[which][index, NV:2 * NV] = low
 
+    @pl.when(jnp.logical_and(relay_left, group > 0))
+    def _():
+        relay_in(1).wait_recv()
+        relay_out(0).start()
+
+    @pl.when(jnp.logical_and(relay_right, group < groups - 1))
+    def _():
+        relay_in(0).wait_recv()
+        relay_out(1).start()
+
     for other in range(1, FOLDS):
         source = (fold + other) % FOLDS
 
@@ -418,7 +456,6 @@
         return jnp.where(has_right if side else has_left, ref[parity, side, b], 0.0)
 
     send(0, NEAR + FAR + RESID)
-    edge_start(3, 4)
 
     for other in range(1, FOLDS):
         @pl.when(reachable(chip, position_of((fold + other) % FOLDS)))
@@ -436,8 +473,7 @@
         prepare_most(side)
 
     def edge_last(side):
-        for copy in edge(1 - side)[2:]:
-            copy.wait_recv()
+        relay_out(side).wait_recv()
         prepare_last(side)
         for copy in edge(side):
             copy.wait_send()
@@ -550,6 +586,18 @@
 
     one_turn(rounds - 1, last_turn=True)
 
+    @pl.when(jnp.logical_and(relay_left, group < groups - 1))
+    def _():
+        relay_in(1).wait_send()
+
+    @pl.when(jnp.logical_and(relay_right, group > 0))
+    def _():
+        relay_in(0).wait_send()
+
+    @pl.when(jnp.logical_or(jnp.logical_and(relay_left, group > 0), jnp.logical_and(relay_right, group < groups - 1)))
+    def _():
+        relay_out(0).wait_send()
+
     for b in range(rows):
         gathered[place * rows + b] = iterate[b] + update[rounds % 2, b]
 
@@ -618,7 +666,7 @@
 
     return pl.pallas_call(
         functools.partial(kernel, rows, groups, depth),
-        out_shape=jax.ShapeDtypeStruct(right_side.shape, f32),
+        out_shape=pltpu.VMEM(right_side.shape, f32),
         in_specs=[anywhere] * 5,
         out_specs=vmem,
         scratch_shapes=[
@@ -631,6 +679,7 @@
             pltpu.VMEM((rows, KB, LANES, LANES), f32),
             pltpu.VMEM((outer - 1, KB, LANES, LANES), f32),
             pltpu.VMEM((outer - 1, KB, LANES, LANES), f32),
+            pltpu.VMEM((KB, LANES, LANES), f32),
             pltpu.VMEM((KB, LANES, LANES), f32),
             pltpu.VMEM((KB, LANES, LANES), f32),
             pltpu.VMEM((rows + 2 * outer, KB * LANES, 2 * LANES), jnp.bfloat16),
@@ -648,7 +697,7 @@
             vectors(2, 2, reach),
             vectors(2, 2, outer),
             vectors(owned),
-            dma((6,)), dma((4,)), dma((4, 2)), dma((4, 2)), dma, dma, dma((8,)), dma((8,)),
+            dma((6,)), dma((4,)), dma((2, 2)), dma((2, 2)), dma((3,)), dma((2,)), dma, dma, dma((8,)), dma((8,)),
             dma((2, 2, 3)), dma((2, 2, 3)), dma((7,)), dma((8,)),
         ],
         compiler_params=pltpu.CompilerParams(collective_id=0, has_side_effects=True),

time: 51.5 us -> 49.1 us (0.953)
  the two profiles are of different devices: /device:TPU:25 before, /device:TPU:27 now
where the time goes in v7:
time: 49.1 us; the launch traced here: 49 us
  Pallas kernels  48.4 us (99%)
  local copies, waits for them, and re-layouts  0.66 us (1%)
    pallas_call x1, Pallas kernels, on_device(): pl.pallas_call(functools.partial(kernel, rows, groups, depth), out_shape=...  48.4 us

profile of v7, /device:TPU:27, one launch (start us, length us, event | category | flops | bytes accessed | tf_op | source)
XLA Modules:
  0.0 49.0 jit_solution(7299109721733203368)
XLA Ops:
  0.0 48.4 %shard_map.55 = f32[16,2048]{1,0:T(8,128)S(1)} custom-call(s32[1,8]{1,0:T(1,128)} %counts_in.1, s32[5,64]{1,0:T(8,128)} %bitcast.1, f32[16,2048]{1,0:T(8,128)} %right_side.1, f32[16,2048]{1,0:T(8,128)} %initial.1, f32[64,5,128,128]{3,2,1,0:T(8,128)} %blocks.1), custom_call_target="tpu_custom_call" | custom-call | tf_op jit(solution)/shard_map/pallas_call | solution.py:667
  48.4 0.7 %copy.7 = f32[16,2048]{1,0:T(8,128)} copy(f32[16,2048]{1,0:T(8,128)S(1)} %shard_map.55) | data formatting | bytes 262144

commit v8 on v7

--- a/solution.py
+++ b/solution.py
@@ -18,6 +18,7 @@
 CHIPS = 4
 DEPTH = 2
 RELAYS = (2, 6)
+EARLY = 2
 
 upper_bound = 4.5
 lower_bound = 1.35
@@ -166,6 +167,7 @@
         refs = [
             (columns, edge_columns.at[target]),
             (blocks.at[pl.ds(begin, most)], (raw_right if target else raw_left)),
+            (blocks.at[begin + most, pl.ds(0, EARLY)], raw_last[target].at[pl.ds(0, EARLY)]),
         ]
         return [
             pltpu.make_async_remote_copy(
@@ -177,13 +179,13 @@
 
     def relay_in(side):
         return pltpu.make_async_remote_copy(
-            src_ref=blocks.at[(owned - outer if side else 0) + most], dst_ref=handed, send_sem=relay_sems.at[0],
+            src_ref=blocks.at[(owned - outer if side else 0) + most, pl.ds(EARLY, KB - EARLY)], dst_ref=handed, send_sem=relay_sems.at[0],
             recv_sem=relay_sems.at[1], device_id=above if side else below, device_id_type=MESH,
         )
 
     def relay_out(side):
         return pltpu.make_async_remote_copy(
-            src_ref=handed, dst_ref=raw_last[side], send_sem=relay_sems.at[2], recv_sem=last_sem.at[side],
+            src_ref=handed, dst_ref=raw_last[side].at[pl.ds(EARLY, KB - EARLY)], send_sem=relay_sems.at[2], recv_sem=last_sem.at[side],
             device_id={"group": group, "fold": fold_of(side * (FOLDS - 1))}, device_id_type=MESH,
         )
 
@@ -473,6 +475,7 @@
         prepare_most(side)
 
     def edge_last(side):
+        edge(1 - side)[2].wait_recv()
         relay_out(side).wait_recv()
         prepare_last(side)
         for copy in edge(side):
@@ -556,14 +559,21 @@
                     finish(j + outer, partial[j] + product(now, j + outer, 0, low))
                 elif high < KB:
                     finish(j + outer, partial[j] + product(now, j + outer, high, KB))
+            def settled(e):
+                return (HB - e, KB) if e < outer else (0, KB - 1 - (e - outer - rows))
+
+            beyond_rows = list(range(outer)) + list(range(outer + rows, wide))
+            if first_turn:
+                at_edges(edge_last)
+            for i, e in enumerate(beyond_rows):
+                partial[i] = product(now, e, *settled(e))
             receive(parity, FAR + given)
             for b in range(reach - HB):
                 store_vector(now, b, halo_of(halo_update, parity, 0, b))
                 store_vector(now, reach + rows + HB + b, halo_of(halo_update, parity, 1, HB + b))
-            if first_turn:
-                at_edges(edge_last)
-            for e in list(range(outer)) + list(range(outer + rows, wide)):
-                finish(e, product(now, e, 0, KB))
+            for i, e in enumerate(beyond_rows):
+                low, high = settled(e)
+                finish(e, partial[i] + (product(now, e, 0, low) if low else product(now, e, high, KB)))
 
         if not last_turn:
             send(1 - parity, FAR)
@@ -608,25 +618,30 @@
             device_id={"group": group, "fold": dest}, device_id_type=MESH,
         )
 
-    def wanted(where, dest, act):
-        @pl.when(reachable(dest // 2, where))
-        def _():
-            act()
-
-    def forward(where, which):
-        piece(where, partner, 0).wait_recv()
-        piece(where, partner, which).start()
-
-    for other in (2, 1, 3):
-        dest = (fold + 2 * other) % FOLDS
-        wanted(place, dest, piece(place, dest, other).start)
-    wanted(place, partner, piece(place, partner, 0).start)
-    for other in (1, 3, 2):
-        where = position_of((fold + 2 * other) % FOLDS)
-        wanted(where, partner, functools.partial(forward, where, 3 + other))
-    for other in range(CHIPS):
-        where = position_of((partner + 2 * other) % FOLDS)
-        wanted(where, fold, piece(where, partner, 0).wait_recv)
+    def needs(dest, where):
+        return jnp.logical_and(where >= 2 * dest - FOLDS, where <= 2 * dest + 1)
+
+    def either(chip_of, where):
+        return jnp.logical_or(needs(chip_of // 2 * 2, where), needs(chip_of // 2 * 2 + 1, where))
+
+    across = (fold + FOLDS // 2) % FOLDS
+    across_partner = (partner + FOLDS // 2) % FOLDS
+    beside_me = {other: (fold + 2 * other) % FOLDS for other in (1, 3)}
+    outgoing = [(2, place, across, needs(across, place)), (5, place, across_partner, needs(across_partner, place))]
+    outgoing += [(other, place, dest, either(dest, place)) for other, dest in beside_me.items()]
+    outgoing += [(0, place, partner, needs(partner, place))]
+    passed_on = [
+        (3 + other, position_of(source), partner, needs(partner, position_of(source))) for other, source in beside_me.items()
+    ]
+
+    for which, where, dest, wish in outgoing:
+        pl.when(wish)(piece(where, dest, which).start)
+    for which, where, dest, wish in passed_on:
+        pl.when(either(fold, where))(piece(where, dest, which).wait_recv)
+        pl.when(wish)(piece(where, dest, which).start)
+    for source in [partner, across, across_partner] + [(partner + 2 * other) % FOLDS for other in (1, 3)]:
+        where = position_of(source)
+        pl.when(needs(fold, where))(piece(where, partner, 0).wait_recv)
 
     begin, live = start_of(fold), count_of(fold)
     shift = begin & (LANES - 1)
@@ -643,10 +658,8 @@
         out[:, m * LANES:(m + 1) * LANES] = jnp.where(lane + m * LANES < live, value, 0.0)
         here = after
 
-    for other in range(CHIPS):
-        wanted(place, (fold + 2 * other) % FOLDS if other else partner, piece(place, partner, other).wait_send)
-        if other:
-            wanted(position_of((fold + 2 * other) % FOLDS), partner, piece(place, partner, 3 + other).wait_send)
+    for which, where, dest, wish in outgoing + passed_on:
+        pl.when(wish)(piece(where, dest, which).wait_send)
 
 
 def on_device(right_side, initial, counts, columns, blocks):
@@ -681,7 +694,7 @@
             pltpu.VMEM((outer - 1, KB, LANES, LANES), f32),
             pltpu.VMEM((KB, LANES, LANES), f32),
             pltpu.VMEM((KB, LANES, LANES), f32),
-            pltpu.VMEM((KB, LANES, LANES), f32),
+            pltpu.VMEM((KB - EARLY, LANES, LANES), f32),
             pltpu.VMEM((rows + 2 * outer, KB * LANES, 2 * LANES), jnp.bfloat16),
             pltpu.SMEM((rows + 2 * outer, KB), i32),
             pltpu.SMEM((3, KB, owned), i32),
@@ -697,7 +710,7 @@
             vectors(2, 2, reach),
             vectors(2, 2, outer),
             vectors(owned),
-            dma((6,)), dma((4,)), dma((2, 2)), dma((2, 2)), dma((3,)), dma((2,)), dma, dma, dma((8,)), dma((8,)),
+            dma((6,)), dma((4,)), dma((3, 2)), dma((3, 2)), dma((3,)), dma((2,)), dma, dma, dma((8,)), dma((8,)),
             dma((2, 2, 3)), dma((2, 2, 3)), dma((7,)), dma((8,)),
         ],
         compiler_params=pltpu.CompilerParams(collective_id=0, has_side_effects=True),

time: 49.1 us -> 47 us (0.957)
  the two profiles are of different devices: /device:TPU:27 before, /device:TPU:25 now
where the time goes in v8:
time: 47 us; the launch traced here: 46.7 us
  Pallas kernels  46.1 us (98%)
  local copies, waits for them, and re-layouts  0.66 us (1%)
    pallas_call x1, Pallas kernels, on_device(): pl.pallas_call(functools.partial(kernel, rows, groups, depth), out_shape=...  46.1 us

profile of v8, /device:TPU:25, one launch (start us, length us, event | category | flops | bytes accessed | tf_op | source)
XLA Modules:
  0.0 46.7 jit_solution(3645435462625535215)
XLA Ops:
  0.0 46.1 %shard_map.55 = f32[16,2048]{1,0:T(8,128)S(1)} custom-call(s32[1,8]{1,0:T(1,128)} %counts_in.1, s32[5,64]{1,0:T(8,128)} %bitcast.1, f32[16,2048]{1,0:T(8,128)} %right_side.1, f32[16,2048]{1,0:T(8,128)} %initial.1, f32[64,5,128,128]{3,2,1,0:T(8,128)} %blocks.1), custom_call_target="tpu_custom_call" | custom-call | tf_op jit(solution)/shard_map/pallas_call | solution.py:680
  46.1 0.7 %copy.7 = f32[16,2048]{1,0:T(8,128)} copy(f32[16,2048]{1,0:T(8,128)S(1)} %shard_map.55) | data formatting | bytes 262144

commit v9 on v8

--- a/solution.py
+++ b/solution.py
@@ -446,16 +446,26 @@
 
         neighbours(act)
 
-    def receive(parity, chosen):
-        def act(sides):
+    primary = place // (FOLDS - 1)
+    secondary = 1 - primary
+
+    def present(side):
+        return jnp.where(side == 0, has_left, has_right)
+
+    def halo_of(ref, parity, side, b):
+        return jnp.where(present(side), ref[parity, side, b], 0.0)
+
+    def send_one(parity, side, chosen):
+        @pl.when(present(side))
+        def _():
             for which in chosen:
-                for side in sides:
-                    exchange(parity, 1 - side, which).wait_recv()
-
-        neighbours(act)
-
-    def halo_of(ref, parity, side, b):
-        return jnp.where(has_right if side else has_left, ref[parity, side, b], 0.0)
+                exchange(parity, side, which).start()
+
+    def receive_one(parity, side, chosen):
+        @pl.when(present(side))
+        def _():
+            for which in chosen:
+                exchange(parity, 1 - side, which).wait_recv()
 
     send(0, NEAR + FAR + RESID)
 
@@ -481,9 +491,10 @@
         for copy in edge(side):
             copy.wait_send()
 
-    def product(which, e, low, high):
-        lhs = jnp.concatenate([vectors[which][order[e, s]] for s in range(low, high)], axis=1)
-        full = jnp.dot(lhs, weights[e, low * LANES:high * LANES, :], preferred_element_type=jnp.float32)
+    def product(which, e, low, length):
+        lhs = jnp.concatenate([vectors[which][order[e, low + s]] for s in range(length)], axis=1)
+        begin = low * LANES if isinstance(low, int) else pl.multiple_of(low * LANES, LANES)
+        full = jnp.dot(lhs, weights[e, pl.ds(begin, length * LANES), :], preferred_element_type=jnp.float32)
         return (full[:NV, :LANES] + full[:NV, LANES:]) + (full[NV:, :LANES] + full[NV:, LANES:])
 
     def own_slots(j):
@@ -499,15 +510,14 @@
             now, later = level % 2, (level + 1) % 2
             keep, gain = keeps[phase * depth + level], gains[phase * depth + level]
 
-            def finish(e, applied):
+            def finish(e, applied, side=None, distance=0):
                 own = e - outer
-                inside = 0 <= own < rows
                 if level > 0:
                     old, left_over = mid_update[e], mid_resid[e]
-                elif inside:
+                elif side is None:
                     old, left_over = update[parity, own], resid[parity, own]
                 else:
-                    side, at = (0, e + HB) if own < 0 else (1, own - rows)
+                    at = (1 - side) * (reach - 1 - distance) + side * distance
                     old = halo_of(halo_update, parity, side, at)
                     if first_turn:
                         left_over = halo_of(halo_resid, parity, side, at - (1 - side) * HB)
@@ -516,7 +526,7 @@
                         left_over = (old - keeps[before] * mid_update[e]) * (1.0 / gains[before])
                 left_over = left_over - applied
                 fresh = keep * old + gain * left_over
-                if inside:
+                if side is None:
                     iterate[own] = iterate[own] + old
                 if level == depth - 1:
                     update[1 - parity, own] = fresh
@@ -526,21 +536,20 @@
                     mid_resid[e] = left_over
                 store_vector(later, e + HB, fresh)
 
-            margin = HB * (depth - 1 - level)
             if level > 0:
-                ends = list(range(HB)) + list(range(rows - HB, rows))
-                for j in ends:
-                    finish(j + outer, product(now, j + outer, 0, KB))
-
-                if not last_turn:
-                    send(1 - parity, NEAR)
+                for side in (primary, secondary):
+                    for i in range(HB):
+                        e = outer + i + side * (rows - 1 - 2 * i)
+                        finish(e, product(now, e, 0, KB))
+                    if not last_turn:
+                        send_one(1 - parity, side, NEAR)
                 for j in range(HB, rows - HB):
                     finish(j + outer, product(now, j + outer, 0, KB))
                 continue
 
             for j in range(rows):
                 low, high = own_slots(j)
-                applied = product(now, j + outer, low, high)
+                applied = product(now, j + outer, low, high - low)
                 if high - low == KB:
                     finish(j + outer, applied)
                 else:
@@ -549,34 +558,32 @@
             if first_turn:
                 at_edges(edge_most)
             sent_all(parity, NEAR + FAR + given)
-            receive(parity, NEAR)
-            for b in range(HB):
-                store_vector(now, reach - HB + b, halo_of(halo_update, parity, 0, reach - HB + b))
-                store_vector(now, reach + rows + b, halo_of(halo_update, parity, 1, b))
-            for j in range(rows):
-                low, high = own_slots(j)
-                if low > 0:
-                    finish(j + outer, partial[j] + product(now, j + outer, 0, low))
-                elif high < KB:
-                    finish(j + outer, partial[j] + product(now, j + outer, high, KB))
-            def settled(e):
-                return (HB - e, KB) if e < outer else (0, KB - 1 - (e - outer - rows))
-
-            beyond_rows = list(range(outer)) + list(range(outer + rows, wide))
-            if first_turn:
-                at_edges(edge_last)
-            for i, e in enumerate(beyond_rows):
-                partial[i] = product(now, e, *settled(e))
-            receive(parity, FAR + given)
-            for b in range(reach - HB):
-                store_vector(now, b, halo_of(halo_update, parity, 0, b))
-                store_vector(now, reach + rows + HB + b, halo_of(halo_update, parity, 1, HB + b))
-            for i, e in enumerate(beyond_rows):
-                low, high = settled(e)
-                finish(e, partial[i] + (product(now, e, 0, low) if low else product(now, e, high, KB)))
+            for side in (secondary, primary):
+                receive_one(parity, side, NEAR)
+                far_side = reach - HB
+                for b in range(HB):
+                    store_vector(now, far_side + b + side * (rows + HB), halo_of(halo_update, parity, side, (1 - side) * far_side + b))
+                for i in range(HB):
+                    j, length = i + side * (rows - 1 - 2 * i), HB - i
+                    finish(j + outer, partial[j] + product(now, j + outer, side * (KB - length), length))
+                if first_turn and side is primary:
+                    at_edges(edge_last)
+
+                def outer_row(i):
+                    return outer - 1 - i + side * (rows + 1 + 2 * i)
+
+                for i in range(outer):
+                    partial[rows + i] = product(now, outer_row(i), (1 - side) * (1 + i), KB - 1 - i)
+                receive_one(parity, side, FAR + given)
+                for b in range(far_side):
+                    store_vector(now, b + side * (reach + rows + HB), halo_of(halo_update, parity, side, side * HB + b))
+                for i in range(outer):
+                    e = outer_row(i)
+                    finish(e, partial[rows + i] + product(now, e, side * (KB - 1 - i), 1 + i), side, i)
 
         if not last_turn:
-            send(1 - parity, FAR)
+            for side in (primary, secondary):
+                send_one(1 - parity, side, FAR)
 
     def at_edges(act):
         @pl.when(left_edge)
@@ -706,7 +713,7 @@
             vectors(rows + 2 * outer),
             vectors(rows + 2 * outer),
             vectors(rows),
-            vectors(rows),
+            vectors(rows + HB),
             vectors(2, 2, reach),
             vectors(2, 2, outer),
             vectors(owned),

time: 47 us -> 49.3 us (1.049)
  the two profiles are of different devices: /device:TPU:25 before, /device:TPU:27 now
where the time goes in v9:
time: 49.3 us; the launch traced here: 49.2 us
  Pallas kernels  48.5 us (98%)
  local copies, waits for them, and re-layouts  0.66 us (1%)
    pallas_call x1, Pallas kernels, on_device(): pl.pallas_call(functools.partial(kernel, rows, groups, depth), out_shape=...  48.5 us

profile of v9, /device:TPU:27, one launch (start us, length us, event | category | flops | bytes accessed | tf_op | source)
XLA Modules:
  0.0 49.2 jit_solution(11926589018517417231)
XLA Ops:
  0.0 48.5 %shard_map.55 = f32[16,2048]{1,0:T(8,128)S(1)} custom-call(s32[1,8]{1,0:T(1,128)} %counts_in.1, s32[5,64]{1,0:T(8,128)} %bitcast.1, f32[16,2048]{1,0:T(8,128)} %right_side.1, f32[16,2048]{1,0:T(8,128)} %initial.1, f32[64,5,128,128]{3,2,1,0:T(8,128)} %blocks.1), custom_call_target="tpu_custom_call" | custom-call | tf_op jit(solution)/shard_map/pallas_call | solution.py:687
  48.5 0.7 %copy.7 = f32[16,2048]{1,0:T(8,128)} copy(f32[16,2048]{1,0:T(8,128)S(1)} %shard_map.55) | data formatting | bytes 262144

commit v10 on v8

--- a/solution.py
+++ b/solution.py
@@ -17,7 +17,7 @@
 FOLDS = 8
 CHIPS = 4
 DEPTH = 2
-RELAYS = (2, 6)
+RELAYS = (3, 7)
 EARLY = 2
 
 upper_bound = 4.5
@@ -420,7 +420,7 @@
     def neighbours(act):
         @pl.when(inside)
         def _():
-            act(range(2))
+            act([place // (FOLDS - 1), 1 - place // (FOLDS - 1)])
 
         @pl.when(jnp.logical_not(has_left))
         def _():
@@ -621,25 +621,12 @@
     def needs(dest, where):
         return jnp.logical_and(where >= 2 * dest - FOLDS, where <= 2 * dest + 1)
 
-    def either(chip_of, where):
-        return jnp.logical_or(needs(chip_of // 2 * 2, where), needs(chip_of // 2 * 2 + 1, where))
-
-    across = (fold + FOLDS // 2) % FOLDS
-    across_partner = (partner + FOLDS // 2) % FOLDS
-    beside_me = {other: (fold + 2 * other) % FOLDS for other in (1, 3)}
-    outgoing = [(2, place, across, needs(across, place)), (5, place, across_partner, needs(across_partner, place))]
-    outgoing += [(other, place, dest, either(dest, place)) for other, dest in beside_me.items()]
-    outgoing += [(0, place, partner, needs(partner, place))]
-    passed_on = [
-        (3 + other, position_of(source), partner, needs(partner, position_of(source))) for other, source in beside_me.items()
-    ]
+    others = [(fold + other) % FOLDS for other in (4, 3, 5, 2, 6, 1, 7)]
+    outgoing = [(i, place, dest, needs(dest, place)) for i, dest in enumerate(others)]
 
     for which, where, dest, wish in outgoing:
         pl.when(wish)(piece(where, dest, which).start)
-    for which, where, dest, wish in passed_on:
-        pl.when(either(fold, where))(piece(where, dest, which).wait_recv)
-        pl.when(wish)(piece(where, dest, which).start)
-    for source in [partner, across, across_partner] + [(partner + 2 * other) % FOLDS for other in (1, 3)]:
+    for source in others:
         where = position_of(source)
         pl.when(needs(fold, where))(piece(where, partner, 0).wait_recv)
 
@@ -658,7 +645,7 @@
         out[:, m * LANES:(m + 1) * LANES] = jnp.where(lane + m * LANES < live, value, 0.0)
         here = after
 
-    for which, where, dest, wish in outgoing + passed_on:
+    for which, where, dest, wish in outgoing:
         pl.when(wish)(piece(where, dest, which).wait_send)
 
 

time: 47 us -> 46.6 us (level)
  Pallas kernels: 46.1 us -> 45.3 us
    pallas_call x1, Pallas kernels: 46.1 us -> 45.3 us  [on_device(): pl.pallas_call(functools.partial(kernel, rows, groups, depth), out_shape=...]
where the time goes in v10:
time: 46.6 us; the launch traced here: 46 us
  Pallas kernels  45.3 us (97%)
  local copies, waits for them, and re-layouts  0.66 us (1%)
    pallas_call x1, Pallas kernels, on_device(): pl.pallas_call(functools.partial(kernel, rows, groups, depth), out_shape=...  45.3 us

profile of v10, /device:TPU:25, one launch (start us, length us, event | category | flops | bytes accessed | tf_op | source)
XLA Modules:
  0.0 46.0 jit_solution(10662539166688315950)
XLA Ops:
  0.0 45.3 %shard_map.55 = f32[16,2048]{1,0:T(8,128)S(1)} custom-call(s32[1,8]{1,0:T(1,128)} %counts_in.1, s32[5,64]{1,0:T(8,128)} %bitcast.1, f32[16,2048]{1,0:T(8,128)} %right_side.1, f32[16,2048]{1,0:T(8,128)} %initial.1, f32[64,5,128,128]{3,2,1,0:T(8,128)} %blocks.1), custom_call_target="tpu_custom_call" | custom-call | tf_op jit(solution)/shard_map/pallas_call | solution.py:667
  45.3 0.7 %copy.7 = f32[16,2048]{1,0:T(8,128)} copy(f32[16,2048]{1,0:T(8,128)S(1)} %shard_map.55) | data formatting | bytes 262144

commit v11 on v10

--- a/solution.py
+++ b/solution.py
@@ -285,7 +285,7 @@
             device_id={"group": group, "fold": fold}, device_id_type=MESH,
         )
 
-    for other in (4, 3, 5, 2, 6, 1, 7):
+    for other in (4, 5, 3, 6, 2, 7, 1):
         where, copy = message(other)
         for b in range(rows):
             sent[where + b] = row_block(where + b)
@@ -340,6 +340,16 @@
     own_blocks.wait()
     prepare(raw_own, outer, outer + rows)
 
+    @pl.when(jnp.logical_and(relay_left, group > 0))
+    def _():
+        relay_in(1).wait_recv()
+        relay_out(0).start()
+
+    @pl.when(jnp.logical_and(relay_right, group < groups - 1))
+    def _():
+        relay_in(0).wait_recv()
+        relay_out(1).start()
+
     def prepare_most(side):
         at = side * (outer + rows)
         prepare(raw_right if side else raw_left, at, at + most)
@@ -376,16 +386,6 @@
         high, low = split(value)
         vectors[which][index, 0:NV] = high
         vectors[which][index, NV:2 * NV] = low
-
-    @pl.when(jnp.logical_and(relay_left, group > 0))
-    def _():
-        relay_in(1).wait_recv()
-        relay_out(0).start()
-
-    @pl.when(jnp.logical_and(relay_right, group < groups - 1))
-    def _():
-        relay_in(0).wait_recv()
-        relay_out(1).start()
 
     for other in range(1, FOLDS):
         source = (fold + other) % FOLDS

time: 46.6 us -> 46.6 us (level)
  no operation moved by 1% of the time
where the time goes in v11:
time: 46.6 us; the launch traced here: 46 us
  Pallas kernels  45.3 us (97%)
  local copies, waits for them, and re-layouts  0.66 us (1%)
    pallas_call x1, Pallas kernels, on_device(): pl.pallas_call(functools.partial(kernel, rows, groups, depth), out_shape=...  45.3 us

profile of v11, /device:TPU:25, one launch (start us, length us, event | category | flops | bytes accessed | tf_op | source)
XLA Modules:
  0.0 46.0 jit_solution(87576178308474932)
XLA Ops:
  0.0 45.3 %shard_map.55 = f32[16,2048]{1,0:T(8,128)S(1)} custom-call(s32[1,8]{1,0:T(1,128)} %counts_in.1, s32[5,64]{1,0:T(8,128)} %bitcast.1, f32[16,2048]{1,0:T(8,128)} %right_side.1, f32[16,2048]{1,0:T(8,128)} %initial.1, f32[64,5,128,128]{3,2,1,0:T(8,128)} %blocks.1), custom_call_target="tpu_custom_call" | custom-call | tf_op jit(solution)/shard_map/pallas_call | solution.py:667
  45.3 0.7 %copy.7 = f32[16,2048]{1,0:T(8,128)} copy(f32[16,2048]{1,0:T(8,128)S(1)} %shard_map.55) | data formatting | bytes 262144

commit v12 on v10

--- a/solution.py
+++ b/solution.py
@@ -18,7 +18,7 @@
 CHIPS = 4
 DEPTH = 2
 RELAYS = (3, 7)
-EARLY = 2
+EARLY = 3
 
 upper_bound = 4.5
 lower_bound = 1.35

time: 46.6 us -> 47.2 us (1.013)
  Pallas kernels: 45.3 us -> 46.4 us
    pallas_call x1, Pallas kernels: 45.3 us -> 46.4 us  [on_device(): pl.pallas_call(functools.partial(kernel, rows, groups, depth), out_shape=...]
where the time goes in v12:
time: 47.2 us; the launch traced here: 47.1 us
  Pallas kernels  46.4 us (98%)
  local copies, waits for them, and re-layouts  0.66 us (1%)
    pallas_call x1, Pallas kernels, on_device(): pl.pallas_call(functools.partial(kernel, rows, groups, depth), out_shape=...  46.4 us

profile of v12, /device:TPU:25, one launch (start us, length us, event | category | flops | bytes accessed | tf_op | source)
XLA Modules:
  0.0 47.1 jit_solution(2759817063650878987)
XLA Ops:
  0.0 46.4 %shard_map.55 = f32[16,2048]{1,0:T(8,128)S(1)} custom-call(s32[1,8]{1,0:T(1,128)} %counts_in.1, s32[5,64]{1,0:T(8,128)} %bitcast.1, f32[16,2048]{1,0:T(8,128)} %right_side.1, f32[16,2048]{1,0:T(8,128)} %initial.1, f32[64,5,128,128]{3,2,1,0:T(8,128)} %blocks.1), custom_call_target="tpu_custom_call" | custom-call | tf_op jit(solution)/shard_map/pallas_call | solution.py:667
  46.4 0.7 %copy.7 = f32[16,2048]{1,0:T(8,128)} copy(f32[16,2048]{1,0:T(8,128)S(1)} %shard_map.55) | data formatting | bytes 262144
